TPU v7x, 1024 devices: a whole 8x8x8 slice. The times are simulated.
1024 devices in a mesh: beam: 16 (over z, core), lat: 64 (over x, y).
Axes of the slice: x: 8, y: 8, z: 8, core: 2. Of those that a mesh axis runs over, the one named last changes fastest.
Arguments:
- contrast: float32 [2, 16, 8192, 256], P(None, 'beam', 'lat'), may hold values from -0.15 to 0.15
- probe: float32 [2, 128, 128], replicated, may hold values from -6 to 6
- offset_x: int32 [512], P('lat'), may hold values from 0 to 127
- offset_y: int32 [512], P('lat'), may hold values from 0 to 128
- probe_count: int32 [64], P('lat'), may hold values from 1 to 8, 384 in all
- measured: float32 [512, 128, 128], P('lat'), may hold values from 0 to 4
Outputs:
- object_gradient: float32 [2, 16, 8192, 256], P(None, 'beam', 'lat')
Inputs may be any that keep to these rules, and one draw needn't show every extreme that they name: `probe_count`: slots below this count hold probes; the others hold none and add nothing; some lat index has all 8. `offset_x`: a probe's block may reach into the next lat index's columns.
All inputs are finite; a program needn't handle non-finite values. No bound on the sum of `probe_count` on one device may be relied on, other than what follows from the above.
Results may differ from a plain program's by a relative error of at most 0.038.
Values may be sent and summed in bfloat16 or wider, within the bound.
A program may use at most 32 MiB of HBM per device.

v0:
```python
import math

import jax
import jax.numpy as jnp
from jax import lax
from jax.sharding import PartitionSpec as P


def shifted_2(value, axis, by):
    length = lax.axis_size(axis)
    pairs = [(i, i + by) for i in range(length) if 0 <= i + by < length]
    return lax.ppermute(value, axis, pairs)


def tables(order):
    index = jnp.arange(order, dtype=jnp.int32)
    product = index[:, None] * index[None, :] % order
    theta = product.astype(jnp.float32) * (2.0 * math.pi / order)
    factor = 1.0 / math.sqrt(order)
    shifted = (index + order // 2) % order - order // 2
    quad = (shifted[:, None] * shifted[:, None] + shifted[None, :] * shifted[None, :]) % (4 * order)
    phase = quad.astype(jnp.float32) * (-math.pi / (2 * order))
    return (jnp.cos(theta) * factor, -jnp.sin(theta) * factor, jnp.cos(phase), jnp.sin(phase))


def left_product(matrix, field):
    return jnp.einsum("mn,...nk->...mk", matrix, field, precision=lax.Precision.HIGHEST)


def right_product(field, matrix):
    return jnp.einsum("...mn,nk->...mk", field, matrix, precision=lax.Precision.HIGHEST)


def both_sides(field_re, field_im, matrix_re, matrix_im):
    half_re = left_product(matrix_re, field_re) - left_product(matrix_im, field_im)
    half_im = left_product(matrix_re, field_im) + left_product(matrix_im, field_re)
    full_re = right_product(half_re, matrix_re) - right_product(half_im, matrix_im)
    full_im = right_product(half_re, matrix_im) + right_product(half_im, matrix_re)
    return (full_re, full_im)


def propagate(field_re, field_im, tabs, sign):
    dft_re, dft_im, kernel_re, kernel_im = tabs
    spec_re, spec_im = both_sides(field_re, field_im, dft_re, dft_im)
    signed_im = sign * kernel_im
    mixed_re = spec_re * kernel_re - spec_im * signed_im
    mixed_im = spec_re * signed_im + spec_im * kernel_re
    return both_sides(mixed_re, mixed_im, dft_re, -dft_im)


def far_field(exit_re, exit_im, observed, live, tabs):
    dft_re, dft_im = (tabs[0], tabs[1])
    far_re, far_im = both_sides(exit_re, exit_im, dft_re, dft_im)
    misfit = live[:, None, None] * (far_re * far_re + far_im * far_im - observed)
    return both_sides(misfit * far_re, misfit * far_im, dft_re, -dft_im)


def on_device(contrast, probe, offset_x, offset_y, probe_count, measured):
    patch_size = probe.shape[1]
    slices = contrast.shape[1]
    tile_cols = contrast.shape[2]
    height = contrast.shape[3]
    slot_count = offset_x.shape[0]
    beam_size = lax.axis_size("beam")
    group_index = lax.axis_index("beam")
    tabs = tables(patch_size)
    anchor = jnp.zeros((), jnp.int32)
    rim_cols = shifted_2(contrast.astype(jnp.bfloat16), "lat", -1).astype(contrast.dtype)
    extended = jnp.concatenate([contrast, rim_cols], axis=2)

    def cut_block(x_start, y_start):
        return lax.dynamic_slice(
            extended, (anchor, anchor, x_start, y_start), (2, slices, patch_size, patch_size)
        )

    patches = jax.vmap(cut_block)(offset_x, offset_y)
    trans_re = 1.0 + jnp.transpose(patches[:, 0], (1, 0, 2, 3))
    trans_im = jnp.transpose(patches[:, 1], (1, 0, 2, 3))
    live_count = probe_count[0]
    live = (jnp.arange(slot_count, dtype=jnp.int32) < live_count).astype(jnp.float32)
    batch_size = 2
    batches = slot_count // batch_size
    steps = beam_size + batches - 1
    block_shape = (batch_size, patch_size, patch_size)

    def take(array, layer_index, first_slot):
        return lax.dynamic_slice(
            array, (jnp.int32(layer_index), first_slot, anchor, anchor), (1,) + block_shape
        )[0]

    def forward_step(step_index, loop_state):
        incoming, kept_re, kept_im, exit_re, exit_im = loop_state
        batch = step_index - group_index
        first_slot = jnp.clip(batch, 0, batches - 1) * batch_size
        active = (batch >= 0) & (batch < batches) & (first_slot < live_count)
        first_wave = jnp.broadcast_to(probe[:, None], (2,) + block_shape)
        wave = jnp.where(group_index == 0, first_wave, incoming.astype(jnp.float32))

        def forward_run_batch(state):
            kept_re, kept_im, exit_re, exit_im = state
            wave_re, wave_im = (wave[0], wave[1])
            place = (jnp.int32(0), first_slot, anchor, anchor)
            kept_re = lax.dynamic_update_slice(kept_re, wave_re[None], place)
            kept_im = lax.dynamic_update_slice(kept_im, wave_im[None], place)
            group_re = take(trans_re, 0, first_slot)
            group_im = take(trans_im, 0, first_slot)
            mult_re = group_re * wave_re - group_im * wave_im
            mult_im = group_re * wave_im + group_im * wave_re
            wave_re, wave_im = propagate(mult_re, mult_im, tabs, 1.0)
            exit_re = lax.dynamic_update_slice(exit_re, wave_re, (first_slot, anchor, anchor))
            exit_im = lax.dynamic_update_slice(exit_im, wave_im, (first_slot, anchor, anchor))
            outgoing = jnp.stack([wave_re, wave_im]).astype(jnp.bfloat16)
            return (kept_re, kept_im, exit_re, exit_im, outgoing)

        def forward_pass_batch(state):
            return state + (jnp.zeros((2,) + block_shape, jnp.bfloat16),)

        kept_re, kept_im, exit_re, exit_im, outgoing = lax.cond(
            active, forward_run_batch, forward_pass_batch, (kept_re, kept_im, exit_re, exit_im)
        )
        incoming = shifted_2(outgoing, "beam", 1)
        return (incoming, kept_re, kept_im, exit_re, exit_im)

    stored_shape = (slices, slot_count, patch_size, patch_size)
    exit_shape = (slot_count, patch_size, patch_size)
    start_state = (
        jnp.zeros((2,) + block_shape, jnp.bfloat16),
        jnp.zeros(stored_shape, jnp.float32),
        jnp.zeros(stored_shape, jnp.float32),
        jnp.zeros(exit_shape, jnp.float32),
        jnp.zeros(exit_shape, jnp.float32),
    )
    unused, kept_re, kept_im, exit_re, exit_im = lax.fori_loop(0, steps, forward_step, start_state)

    def final_far(state):
        return far_field(state[0], state[1], measured, live, tabs)

    def empty_far(state):
        return (jnp.zeros(exit_shape, jnp.float32), jnp.zeros(exit_shape, jnp.float32))

    last_re, last_im = lax.cond(
        group_index == beam_size - 1, final_far, empty_far, (exit_re, exit_im)
    )
    last_adjoint = jnp.stack([last_re, last_im])

    def back_step(step_index, loop_state):
        incoming, grad_re, grad_im = loop_state
        batch = step_index - (beam_size - 1 - group_index)
        first_slot = jnp.clip(batch, 0, batches - 1) * batch_size
        active = (batch >= 0) & (batch < batches) & (first_slot < live_count)
        own_adjoint = lax.dynamic_slice_in_dim(last_adjoint, first_slot, batch_size, 1)
        adjoint = jnp.where(group_index == beam_size - 1, own_adjoint, incoming.astype(jnp.float32))

        def back_run_batch(state):
            grad_re, grad_im = state
            adj_re, adj_im = (adjoint[0], adjoint[1])
            for layer_index in reversed(range(slices)):
                back_re, back_im = propagate(adj_re, adj_im, tabs, -1.0)
                psi_re = take(kept_re, layer_index, first_slot)
                psi_im = take(kept_im, layer_index, first_slot)
                place = (jnp.int32(layer_index), first_slot, anchor, anchor)
                grad_re = lax.dynamic_update_slice(
                    grad_re, (psi_re * back_re + psi_im * back_im)[None], place
                )
                grad_im = lax.dynamic_update_slice(
                    grad_im, (psi_re * back_im - psi_im * back_re)[None], place
                )
                group_re = take(trans_re, layer_index, first_slot)
                group_im = take(trans_im, layer_index, first_slot)
                adj_re, adj_im = (
                    group_re * back_re + group_im * back_im,
                    group_re * back_im - group_im * back_re,
                )
            outgoing = jnp.stack([adj_re, adj_im]).astype(jnp.bfloat16)
            return (grad_re, grad_im, outgoing)

        def back_pass_batch(state):
            return state + (jnp.zeros((2,) + block_shape, jnp.bfloat16),)

        grad_re, grad_im, outgoing = lax.cond(
            active, back_run_batch, back_pass_batch, (grad_re, grad_im)
        )
        incoming = shifted_2(outgoing, "beam", -1)
        return (incoming, grad_re, grad_im)

    back_state = (
        jnp.zeros((2,) + block_shape, jnp.bfloat16),
        jnp.zeros(stored_shape, jnp.float32),
        jnp.zeros(stored_shape, jnp.float32),
    )
    unused, grad_re, grad_im = lax.fori_loop(0, steps, back_step, back_state)
    grad_ext = jnp.zeros((2, slices, tile_cols + patch_size, height), jnp.float32)
    for slot_index in range(slot_count):
        piece = jnp.stack([grad_re[:, slot_index], grad_im[:, slot_index]])
        place = (anchor, anchor, offset_x[slot_index], offset_y[slot_index])
        current = lax.dynamic_slice(grad_ext, place, piece.shape)
        grad_ext = lax.dynamic_update_slice(grad_ext, current + piece, place)
    arrived = shifted_2(grad_ext[:, :, tile_cols:].astype(jnp.bfloat16), "lat", 1).astype(
        jnp.float32
    )
    own_cols = grad_ext[:, :, :tile_cols]
    return own_cols.at[:, :, :patch_size].add(arrived)


def solution(mesh):
    in_specs = (
        P(None, "beam", "lat", None),
        P(),
        P("lat"),
        P("lat"),
        P("lat"),
        P("lat", None, None),
    )
    out_specs = P(None, "beam", "lat", None)
    return jax.shard_map(
        on_device, mesh=mesh, in_specs=in_specs, out_specs=out_specs, check_vma=False
    )
```

profile of v0, /device:TPU:16, one launch (start us, length us, event | category | flops | bytes accessed | tf_op | source)
XLA Modules:
  0.0 668.1 jit_solution(8313266842607878506)
XLA Ops:
  1.0 15.0 %collective-permute-start.2 = (bf16[2,1,128,256]{3,2,1,0:T(8,128)(2,1)S(1)}, bf16[2,1,128,256]{3,2,1,0:T(8,128)(2,1)S(1)}, u32[]{:S(2)}, u32[]{:S(2)}) collective-permute-start(bf16[2,1,128,256]{3,2,1,0:T(8,128)(2,1)S(1)} %convert_element_type.169), channel_id=1, source_target_pairs={{1,0},{2,1},{3,2},{4,3},{5,4},{6,5},{7,6},{8,7},{9,8},{10,9},{11,1... | collective-permute-start | bytes 393224 | tf_op jit(solution)/shard_map/ppermute | solution.py:12
  48.0 16.1 %while.50 = (s32[]{:T(128)}, f32[2,1,256,256]{3,2,1,0:T(8,128)S(1)}, s32[8,4]{0,1:T(4,128)S(1)}, f32[8,2,1,128,128]{4,3,0,2,1:T(8,128)S(1)}, s32[]{:T(128)}) while((s32[]{:T(128)}, f32[2,1,256,256]{3,2,1,0:T(8,128)S(1)}, s32[8,4]{0,1:T(4,128)S(1)}, f32[8,2,1,128,128]{4,3,0,2,1:T(8,128)S(1)}, s32[]{:T(128)}) %tuple.262), condition=%wide.while_cond.1, body=%wide.while_body.1.sunk | while | flops 2 | bytes 262269 | solution.py:72
  67.2 208.4 %while.51 = (s32[]{:T(128)}, bf16[2,2,128,128]{3,2,1,0:T(8,128)(2,1)S(1)}, f32[1,8,128,128]{2,3,1,0:T(8,128)}, f32[1,8,128,128]{2,3,1,0:T(8,128)}, f32[8,128,128...) while((s32[]{:T(128)}, ...), condition=%wide.region_3.4_spmd.clone.clone.clone, body=%wide.region_0.3_spmd.clone.clone.clone.sunk | while | flops 806993920 | bytes 11207714 | solution.py:133
  68.0 8.7 %conditional.12 = (f32[1,8,128,128]{2,3,1,0:T(8,128)}, f32[1,8,128,128]{2,3,1,0:T(8,128)}, f32[8,128,128]{2,1,0:T(8,128)S(1)}, f32[8,128,128]{2,1,0:T(8,128)S(1)}, bf16[2,2,128,128]{3,2,1,0:T(8,128)(2,1)S(1)}) conditional(s32[]{:T(128)} %convert_element_type.248, (f32[1,8,128,128]{2,3,1,0:T(8,128)}, f32[1,8,128,128]{2,3,1,0:T(8,128)}, ...), branch_computations={%region_1.1_spmd, %region_2.2_spmd.clone} | conditional | flops 806535168 | bytes 10485843 | solution.py:118
  79.8 8.8 %conditional.12 = (f32[1,8,128,128]{2,3,1,0:T(8,128)}, f32[1,8,128,128]{2,3,1,0:T(8,128)}, f32[8,128,128]{2,1,0:T(8,128)S(1)}, f32[8,128,128]{2,1,0:T(8,128)S(1)}, bf16[2,2,128,128]{3,2,1,0:T(8,128)(2,1)S(1)}) conditional(s32[]{:T(128)} %convert_element_type.248, (f32[1,8,128,128]{2,3,1,0:T(8,128)}, f32[1,8,128,128]{2,3,1,0:T(8,128)}, ...), branch_computations={%region_1.1_spmd, %region_2.2_spmd.clone} | conditional | flops 806535168 | bytes 10485843 | solution.py:118
  80.0 1.7 multiply_add_fusion.1
  88.5 2.2 collective-permute-start
  92.5 8.8 %conditional.12 = (f32[1,8,128,128]{2,3,1,0:T(8,128)}, f32[1,8,128,128]{2,3,1,0:T(8,128)}, f32[8,128,128]{2,1,0:T(8,128)S(1)}, f32[8,128,128]{2,1,0:T(8,128)S(1)}, bf16[2,2,128,128]{3,2,1,0:T(8,128)(2,1)S(1)}) conditional(s32[]{:T(128)} %convert_element_type.248, (f32[1,8,128,128]{2,3,1,0:T(8,128)}, f32[1,8,128,128]{2,3,1,0:T(8,128)}, ...), branch_computations={%region_1.1_spmd, %region_2.2_spmd.clone} | conditional | flops 806535168 | bytes 10485843 | solution.py:118
  101.3 2.9 collective-permute-start
  105.9 8.7 %conditional.12 = (f32[1,8,128,128]{2,3,1,0:T(8,128)}, f32[1,8,128,128]{2,3,1,0:T(8,128)}, f32[8,128,128]{2,1,0:T(8,128)S(1)}, f32[8,128,128]{2,1,0:T(8,128)S(1)}, bf16[2,2,128,128]{3,2,1,0:T(8,128)(2,1)S(1)}) conditional(s32[]{:T(128)} %convert_element_type.248, (f32[1,8,128,128]{2,3,1,0:T(8,128)}, f32[1,8,128,128]{2,3,1,0:T(8,128)}, ...), branch_computations={%region_1.1_spmd, %region_2.2_spmd.clone} | conditional | flops 806535168 | bytes 10485843 | solution.py:118
  114.7 5.3 collective-permute-start
  121.8 14.0 %collective-permute-start = (bf16[2,2,128,128]{3,2,1,0:T(8,128)(2,1)S(1)}, bf16[2,2,128,128]{3,2,1,0:T(8,128)(2,1)S(1)}, u32[]{:S(2)}, u32[]{:S(2)}) collective-permute-start(bf16[2,2,128,128]{3,2,1,0:T(8,128)(2,1)S(1)} %get-tuple-element.1888), channel_id=1, source_target_pairs={{0,64},{64,128},{128,192},{192,256},{256,320},{320,384},{384,448},... | collective-permute-start | bytes 393224 | tf_op jit(solution)/shard_map/while/body/eval_jaxpr/ppermute | solution.py:12
  137.6 5.4 collective-permute-start
  144.8 14.0 %collective-permute-start = (bf16[2,2,128,128]{3,2,1,0:T(8,128)(2,1)S(1)}, bf16[2,2,128,128]{3,2,1,0:T(8,128)(2,1)S(1)}, u32[]{:S(2)}, u32[]{:S(2)}) collective-permute-start(bf16[2,2,128,128]{3,2,1,0:T(8,128)(2,1)S(1)} %get-tuple-element.1888), channel_id=1, source_target_pairs={{0,64},{64,128},{128,192},{192,256},{256,320},{320,384},{384,448},... | collective-permute-start | bytes 393224 | tf_op jit(solution)/shard_map/while/body/eval_jaxpr/ppermute | solution.py:12
  160.6 5.3 collective-permute-start
  167.7 7.6 %collective-permute-start = (bf16[2,2,128,128]{3,2,1,0:T(8,128)(2,1)S(1)}, bf16[2,2,128,128]{3,2,1,0:T(8,128)(2,1)S(1)}, u32[]{:S(2)}, u32[]{:S(2)}) collective-permute-start(bf16[2,2,128,128]{3,2,1,0:T(8,128)(2,1)S(1)} %get-tuple-element.1888), channel_id=1, source_target_pairs={{0,64},{64,128},{128,192},{192,256},{256,320},{320,384},{384,448},... | collective-permute-start | bytes 393224 | tf_op jit(solution)/shard_map/while/body/eval_jaxpr/ppermute | solution.py:12
  177.1 5.3 collective-permute-start
  184.2 11.6 %collective-permute-start = (bf16[2,2,128,128]{3,2,1,0:T(8,128)(2,1)S(1)}, bf16[2,2,128,128]{3,2,1,0:T(8,128)(2,1)S(1)}, u32[]{:S(2)}, u32[]{:S(2)}) collective-permute-start(bf16[2,2,128,128]{3,2,1,0:T(8,128)(2,1)S(1)} %get-tuple-element.1888), channel_id=1, source_target_pairs={{0,64},{64,128},{128,192},{192,256},{256,320},{320,384},{384,448},... | collective-permute-start | bytes 393224 | tf_op jit(solution)/shard_map/while/body/eval_jaxpr/ppermute | solution.py:12
  197.6 5.3 collective-permute-start
  204.8 7.6 %collective-permute-start = (bf16[2,2,128,128]{3,2,1,0:T(8,128)(2,1)S(1)}, bf16[2,2,128,128]{3,2,1,0:T(8,128)(2,1)S(1)}, u32[]{:S(2)}, u32[]{:S(2)}) collective-permute-start(bf16[2,2,128,128]{3,2,1,0:T(8,128)(2,1)S(1)} %get-tuple-element.1888), channel_id=1, source_target_pairs={{0,64},{64,128},{128,192},{192,256},{256,320},{320,384},{384,448},... | collective-permute-start | bytes 393224 | tf_op jit(solution)/shard_map/while/body/eval_jaxpr/ppermute | solution.py:12
  214.1 5.3 collective-permute-start
  221.3 11.6 %collective-permute-start = (bf16[2,2,128,128]{3,2,1,0:T(8,128)(2,1)S(1)}, bf16[2,2,128,128]{3,2,1,0:T(8,128)(2,1)S(1)}, u32[]{:S(2)}, u32[]{:S(2)}) collective-permute-start(bf16[2,2,128,128]{3,2,1,0:T(8,128)(2,1)S(1)} %get-tuple-element.1888), channel_id=1, source_target_pairs={{0,64},{64,128},{128,192},{192,256},{256,320},{320,384},{384,448},... | collective-permute-start | bytes 393224 | tf_op jit(solution)/shard_map/while/body/eval_jaxpr/ppermute | solution.py:12
  234.7 5.3 collective-permute-start
  241.8 7.6 %collective-permute-start = (bf16[2,2,128,128]{3,2,1,0:T(8,128)(2,1)S(1)}, bf16[2,2,128,128]{3,2,1,0:T(8,128)(2,1)S(1)}, u32[]{:S(2)}, u32[]{:S(2)}) collective-permute-start(bf16[2,2,128,128]{3,2,1,0:T(8,128)(2,1)S(1)} %get-tuple-element.1888), channel_id=1, source_target_pairs={{0,64},{64,128},{128,192},{192,256},{256,320},{320,384},{384,448},... | collective-permute-start | bytes 393224 | tf_op jit(solution)/shard_map/while/body/eval_jaxpr/ppermute | solution.py:12
  251.2 6.3 collective-permute-start
  259.4 15.2 %collective-permute-start = (bf16[2,2,128,128]{3,2,1,0:T(8,128)(2,1)S(1)}, bf16[2,2,128,128]{3,2,1,0:T(8,128)(2,1)S(1)}, u32[]{:S(2)}, u32[]{:S(2)}) collective-permute-start(bf16[2,2,128,128]{3,2,1,0:T(8,128)(2,1)S(1)} %get-tuple-element.1888), channel_id=1, source_target_pairs={{0,64},{64,128},{128,192},{192,256},{256,320},{320,384},{384,448},... | collective-permute-start | bytes 393224 | tf_op jit(solution)/shard_map/while/body/eval_jaxpr/ppermute | solution.py:12
  277.8 1.7 conditional.3
  282.5 356.6 %while.52 = (s32[]{:T(128)}, bf16[2,2,128,128]{3,2,1,0:T(8,128)(2,1)S(1)}, f32[1,8,128,128]{3,2,1,0:T(8,128)}, f32[1,8,128,128]{3,2,1,0:T(8,128)}, s32[]{:T(128)...) while((s32[]{:T(128)}, ...), condition=%wide.region_9.10_spmd.clone.clone.clone, body=%wide.region_6.9_spmd.clone.clone.clone.sunk | while | flops 807206912 | bytes 11207686 | solution.py:191
  284.7 6.1 collective-permute-done.1
  292.9 6.9 %collective-permute-done.1 = bf16[2,2,128,128]{3,2,1,0:T(8,128)(2,1)S(1)} collective-permute-done((bf16[2,2,128,128]{3,2,1,0:T(8,128)(2,1)S(1)}, bf16[2,2,128,128]{3,2,1,0:T(8,128)(2,1)S(1)}, u32[]{:S(2)}, u32[]{:S(2)}) %collective-permute-start.1) | collective-permute-done | bytes 131104 | tf_op jit(solution)/shard_map/while/body/eval_jaxpr/ppermute | solution.py:12
  301.9 6.1 collective-permute-done.1
  310.1 10.5 %collective-permute-done.1 = bf16[2,2,128,128]{3,2,1,0:T(8,128)(2,1)S(1)} collective-permute-done((bf16[2,2,128,128]{3,2,1,0:T(8,128)(2,1)S(1)}, bf16[2,2,128,128]{3,2,1,0:T(8,128)(2,1)S(1)}, u32[]{:S(2)}, u32[]{:S(2)}) %collective-permute-start.1) | collective-permute-done | bytes 131104 | tf_op jit(solution)/shard_map/while/body/eval_jaxpr/ppermute | solution.py:12
  322.8 6.1 collective-permute-done.1
  331.0 6.9 %collective-permute-done.1 = bf16[2,2,128,128]{3,2,1,0:T(8,128)(2,1)S(1)} collective-permute-done((bf16[2,2,128,128]{3,2,1,0:T(8,128)(2,1)S(1)}, bf16[2,2,128,128]{3,2,1,0:T(8,128)(2,1)S(1)}, u32[]{:S(2)}, u32[]{:S(2)}) %collective-permute-start.1) | collective-permute-done | bytes 131104 | tf_op jit(solution)/shard_map/while/body/eval_jaxpr/ppermute | solution.py:12
  340.1 6.1 collective-permute-done.1
  348.3 10.5 %collective-permute-done.1 = bf16[2,2,128,128]{3,2,1,0:T(8,128)(2,1)S(1)} collective-permute-done((bf16[2,2,128,128]{3,2,1,0:T(8,128)(2,1)S(1)}, bf16[2,2,128,128]{3,2,1,0:T(8,128)(2,1)S(1)}, u32[]{:S(2)}, u32[]{:S(2)}) %collective-permute-start.1) | collective-permute-done | bytes 131104 | tf_op jit(solution)/shard_map/while/body/eval_jaxpr/ppermute | solution.py:12
  361.0 6.2 collective-permute-done.1
  369.3 6.6 collective-permute-done.1
  378.0 6.2 collective-permute-done.1
  386.4 10.6 %collective-permute-done.1 = bf16[2,2,128,128]{3,2,1,0:T(8,128)(2,1)S(1)} collective-permute-done((bf16[2,2,128,128]{3,2,1,0:T(8,128)(2,1)S(1)}, bf16[2,2,128,128]{3,2,1,0:T(8,128)(2,1)S(1)}, u32[]{:S(2)}, u32[]{:S(2)}) %collective-permute-start.1) | collective-permute-done | bytes 131104 | tf_op jit(solution)/shard_map/while/body/eval_jaxpr/ppermute | solution.py:12
  399.1 6.2 collective-permute-done.1
  407.5 6.6 collective-permute-done.1
  416.2 159.0 %collective-permute-done.1 = bf16[2,2,128,128]{3,2,1,0:T(8,128)(2,1)S(1)} collective-permute-done((bf16[2,2,128,128]{3,2,1,0:T(8,128)(2,1)S(1)}, bf16[2,2,128,128]{3,2,1,0:T(8,128)(2,1)S(1)}, u32[]{:S(2)}, u32[]{:S(2)}) %collective-permute-start.1) | collective-permute-done | bytes 131104 | tf_op jit(solution)/shard_map/while/body/eval_jaxpr/ppermute | solution.py:12
  576.0 8.7 %conditional.13 = (f32[1,8,128,128]{3,2,1,0:T(8,128)}, f32[1,8,128,128]{3,2,1,0:T(8,128)}, bf16[2,2,128,128]{3,2,1,0:T(8,128)(2,1)S(1)}) conditional(s32[]{:T(128)} %convert_element_type.250, (f32[1,8,128,128]{3,2,1,0:T(8,128)}, f32[1,8,128,128]{3,2,1,0:T(8,128)}) %tuple.256, (s32[]{:T(128)}, f32[1,8,128,128]{3,2,1,0:T(8,128)S(1)}, pred[]{:T(512)}, ...), branch_computations={%region_7.7_spmd, %region_8.8_spmd.clone} | conditional | flops 806748160 | bytes 10485831 | solution.py:180
  582.6 2.0 bitcast_dynamic-update-slice_fusion.1
  586.0 6.5 collective-permute-done.1
  593.3 8.7 %conditional.13 = (f32[1,8,128,128]{3,2,1,0:T(8,128)}, f32[1,8,128,128]{3,2,1,0:T(8,128)}, bf16[2,2,128,128]{3,2,1,0:T(8,128)(2,1)S(1)}) conditional(s32[]{:T(128)} %convert_element_type.250, (f32[1,8,128,128]{3,2,1,0:T(8,128)}, f32[1,8,128,128]{3,2,1,0:T(8,128)}) %tuple.256, (s32[]{:T(128)}, f32[1,8,128,128]{3,2,1,0:T(8,128)S(1)}, pred[]{:T(512)}, ...), branch_computations={%region_7.7_spmd, %region_8.8_spmd.clone} | conditional | flops 806748160 | bytes 10485831 | solution.py:180
  599.9 2.0 bitcast_dynamic-update-slice_fusion.1
  603.3 6.1 collective-permute-done.1
  610.2 8.7 %conditional.13 = (f32[1,8,128,128]{3,2,1,0:T(8,128)}, f32[1,8,128,128]{3,2,1,0:T(8,128)}, bf16[2,2,128,128]{3,2,1,0:T(8,128)(2,1)S(1)}) conditional(s32[]{:T(128)} %convert_element_type.250, (f32[1,8,128,128]{3,2,1,0:T(8,128)}, f32[1,8,128,128]{3,2,1,0:T(8,128)}) %tuple.256, (s32[]{:T(128)}, f32[1,8,128,128]{3,2,1,0:T(8,128)S(1)}, pred[]{:T(512)}, ...), branch_computations={%region_7.7_spmd, %region_8.8_spmd.clone} | conditional | flops 806748160 | bytes 10485831 | solution.py:180
  616.9 2.0 bitcast_dynamic-update-slice_fusion.1
  620.3 6.1 collective-permute-done.1
  627.1 8.7 %conditional.13 = (f32[1,8,128,128]{3,2,1,0:T(8,128)}, f32[1,8,128,128]{3,2,1,0:T(8,128)}, bf16[2,2,128,128]{3,2,1,0:T(8,128)(2,1)S(1)}) conditional(s32[]{:T(128)} %convert_element_type.250, (f32[1,8,128,128]{3,2,1,0:T(8,128)}, f32[1,8,128,128]{3,2,1,0:T(8,128)}) %tuple.256, (s32[]{:T(128)}, f32[1,8,128,128]{3,2,1,0:T(8,128)S(1)}, pred[]{:T(512)}, ...), branch_computations={%region_7.7_spmd, %region_8.8_spmd.clone} | conditional | flops 806748160 | bytes 10485831 | solution.py:180
  633.7 2.0 bitcast_dynamic-update-slice_fusion.1
  637.1 1.9 collective-permute-done.1
  641.3 2.4 dynamic_update_slice.44
  643.8 2.3 dynamic_update_slice.45
  646.2 2.3 dynamic_update_slice.46
  648.7 2.5 dynamic_update_slice.47
  651.3 2.5 dynamic_update_slice.48
  653.9 2.1 dynamic_update_slice.49
  657.6 2.3 dynamic_update_slice.51
  660.0 1.9 collective-permute-start.3
  661.9 5.5 collective-permute-done.3
  (438 shorter events, 142.6 us)
Async XLA Ops:
  0.0 16.1 %copy-start.4 = (s32[8]{0:T(128)S(1)}, s32[8]{0:T(128)}, u32[]{:S(2)}) copy-start(s32[8]{0:T(128)} %param.22) | copy-start | bytes 100
  0.0 16.7 %copy-start.5 = (s32[8]{0:T(128)S(1)}, s32[8]{0:T(128)}, u32[]{:S(2)}) copy-start(s32[8]{0:T(128)} %param.23) | copy-start | bytes 100
  1.0 36.8 %copy-start.3 = (f32[2,128,128]{2,1,0:T(8,128)S(1)}, f32[2,128,128]{2,1,0:T(8,128)}, u32[]{:S(2)}) copy-start(f32[2,128,128]{2,1,0:T(8,128)} %param.21) | copy-start | bytes 393220
  1.0 46.9 %collective-permute-start.2 = (bf16[2,1,128,256]{3,2,1,0:T(8,128)(2,1)S(1)}, bf16[2,1,128,256]{3,2,1,0:T(8,128)(2,1)S(1)}, u32[]{:S(2)}, u32[]{:S(2)}) collective-permute-start(bf16[2,1,128,256]{3,2,1,0:T(8,128)(2,1)S(1)} %convert_element_type.169), channel_id=1, source_target_pairs={{1,0},{2,1},{3,2},{4,3},{5,4},{6,5},{7,6},{8,7},{9,8},{10,9},{11,1... | collective-permute-start | bytes 393224 | tf_op jit(solution)/shard_map/ppermute | solution.py:12
  38.0 10.0 %copy-start.1 = (f32[2,1,128,256]{3,2,1,0:T(8,128)S(1)}, f32[2,1,128,256]{3,2,1,0:T(8,128)}, u32[]{:S(2)}) copy-start(f32[2,1,128,256]{3,2,1,0:T(8,128)} %param.20) | copy-start | bytes 786436
  76.7 2.3 collective-permute-start
  88.5 3.2 collective-permute-start
  101.3 3.9 collective-permute-start
  114.7 6.3 collective-permute-start
  121.8 15.0 %collective-permute-start = (bf16[2,2,128,128]{3,2,1,0:T(8,128)(2,1)S(1)}, bf16[2,2,128,128]{3,2,1,0:T(8,128)(2,1)S(1)}, u32[]{:S(2)}, u32[]{:S(2)}) collective-permute-start(bf16[2,2,128,128]{3,2,1,0:T(8,128)(2,1)S(1)} %get-tuple-element.1888), channel_id=1, source_target_pairs={{0,64},{64,128},{128,192},{192,256},{256,320},{320,384},{384,448},... | collective-permute-start | bytes 393224 | tf_op jit(solution)/shard_map/while/body/eval_jaxpr/ppermute | solution.py:12
  137.6 6.3 collective-permute-start
  144.8 15.0 %collective-permute-start = (bf16[2,2,128,128]{3,2,1,0:T(8,128)(2,1)S(1)}, bf16[2,2,128,128]{3,2,1,0:T(8,128)(2,1)S(1)}, u32[]{:S(2)}, u32[]{:S(2)}) collective-permute-start(bf16[2,2,128,128]{3,2,1,0:T(8,128)(2,1)S(1)} %get-tuple-element.1888), channel_id=1, source_target_pairs={{0,64},{64,128},{128,192},{192,256},{256,320},{320,384},{384,448},... | collective-permute-start | bytes 393224 | tf_op jit(solution)/shard_map/while/body/eval_jaxpr/ppermute | solution.py:12
  160.6 6.3 collective-permute-start
  167.7 8.5 %collective-permute-start = (bf16[2,2,128,128]{3,2,1,0:T(8,128)(2,1)S(1)}, bf16[2,2,128,128]{3,2,1,0:T(8,128)(2,1)S(1)}, u32[]{:S(2)}, u32[]{:S(2)}) collective-permute-start(bf16[2,2,128,128]{3,2,1,0:T(8,128)(2,1)S(1)} %get-tuple-element.1888), channel_id=1, source_target_pairs={{0,64},{64,128},{128,192},{192,256},{256,320},{320,384},{384,448},... | collective-permute-start | bytes 393224 | tf_op jit(solution)/shard_map/while/body/eval_jaxpr/ppermute | solution.py:12
  177.1 6.3 collective-permute-start
  184.2 12.6 %collective-permute-start = (bf16[2,2,128,128]{3,2,1,0:T(8,128)(2,1)S(1)}, bf16[2,2,128,128]{3,2,1,0:T(8,128)(2,1)S(1)}, u32[]{:S(2)}, u32[]{:S(2)}) collective-permute-start(bf16[2,2,128,128]{3,2,1,0:T(8,128)(2,1)S(1)} %get-tuple-element.1888), channel_id=1, source_target_pairs={{0,64},{64,128},{128,192},{192,256},{256,320},{320,384},{384,448},... | collective-permute-start | bytes 393224 | tf_op jit(solution)/shard_map/while/body/eval_jaxpr/ppermute | solution.py:12
  197.6 6.3 collective-permute-start
  204.8 8.5 %collective-permute-start = (bf16[2,2,128,128]{3,2,1,0:T(8,128)(2,1)S(1)}, bf16[2,2,128,128]{3,2,1,0:T(8,128)(2,1)S(1)}, u32[]{:S(2)}, u32[]{:S(2)}) collective-permute-start(bf16[2,2,128,128]{3,2,1,0:T(8,128)(2,1)S(1)} %get-tuple-element.1888), channel_id=1, source_target_pairs={{0,64},{64,128},{128,192},{192,256},{256,320},{320,384},{384,448},... | collective-permute-start | bytes 393224 | tf_op jit(solution)/shard_map/while/body/eval_jaxpr/ppermute | solution.py:12
  214.1 6.3 collective-permute-start
  221.3 12.6 %collective-permute-start = (bf16[2,2,128,128]{3,2,1,0:T(8,128)(2,1)S(1)}, bf16[2,2,128,128]{3,2,1,0:T(8,128)(2,1)S(1)}, u32[]{:S(2)}, u32[]{:S(2)}) collective-permute-start(bf16[2,2,128,128]{3,2,1,0:T(8,128)(2,1)S(1)} %get-tuple-element.1888), channel_id=1, source_target_pairs={{0,64},{64,128},{128,192},{192,256},{256,320},{320,384},{384,448},... | collective-permute-start | bytes 393224 | tf_op jit(solution)/shard_map/while/body/eval_jaxpr/ppermute | solution.py:12
  234.7 6.3 collective-permute-start
  241.8 8.5 %collective-permute-start = (bf16[2,2,128,128]{3,2,1,0:T(8,128)(2,1)S(1)}, bf16[2,2,128,128]{3,2,1,0:T(8,128)(2,1)S(1)}, u32[]{:S(2)}, u32[]{:S(2)}) collective-permute-start(bf16[2,2,128,128]{3,2,1,0:T(8,128)(2,1)S(1)} %get-tuple-element.1888), channel_id=1, source_target_pairs={{0,64},{64,128},{128,192},{192,256},{256,320},{320,384},{384,448},... | collective-permute-start | bytes 393224 | tf_op jit(solution)/shard_map/while/body/eval_jaxpr/ppermute | solution.py:12
  251.2 7.3 %collective-permute-start = (bf16[2,2,128,128]{3,2,1,0:T(8,128)(2,1)S(1)}, bf16[2,2,128,128]{3,2,1,0:T(8,128)(2,1)S(1)}, u32[]{:S(2)}, u32[]{:S(2)}) collective-permute-start(bf16[2,2,128,128]{3,2,1,0:T(8,128)(2,1)S(1)} %get-tuple-element.1888), channel_id=1, source_target_pairs={{0,64},{64,128},{128,192},{192,256},{256,320},{320,384},{384,448},... | collective-permute-start | bytes 393224 | tf_op jit(solution)/shard_map/while/body/eval_jaxpr/ppermute | solution.py:12
  259.4 16.2 %collective-permute-start = (bf16[2,2,128,128]{3,2,1,0:T(8,128)(2,1)S(1)}, bf16[2,2,128,128]{3,2,1,0:T(8,128)(2,1)S(1)}, u32[]{:S(2)}, u32[]{:S(2)}) collective-permute-start(bf16[2,2,128,128]{3,2,1,0:T(8,128)(2,1)S(1)} %get-tuple-element.1888), channel_id=1, source_target_pairs={{0,64},{64,128},{128,192},{192,256},{256,320},{320,384},{384,448},... | collective-permute-start | bytes 393224 | tf_op jit(solution)/shard_map/while/body/eval_jaxpr/ppermute | solution.py:12
  275.5 1.3 copy-start
  283.4 7.4 %collective-permute-start.1 = (bf16[2,2,128,128]{3,2,1,0:T(8,128)(2,1)S(1)}, bf16[2,2,128,128]{3,2,1,0:T(8,128)(2,1)S(1)}, u32[]{:S(2)}, u32[]{:S(2)}) collective-permute-start(bf16[2,2,128,128]{3,2,1,0:T(8,128)(2,1)S(1)} %get-tuple-element.1908), channel_id=1, source_target_pairs={{64,0},{128,64},{192,128},{256,192},{320,256},{384,320},{448,384},... | collective-permute-start | bytes 393224 | tf_op jit(solution)/shard_map/while/body/eval_jaxpr/ppermute | solution.py:12
  291.6 8.2 %collective-permute-start.1 = (bf16[2,2,128,128]{3,2,1,0:T(8,128)(2,1)S(1)}, bf16[2,2,128,128]{3,2,1,0:T(8,128)(2,1)S(1)}, u32[]{:S(2)}, u32[]{:S(2)}) collective-permute-start(bf16[2,2,128,128]{3,2,1,0:T(8,128)(2,1)S(1)} %get-tuple-element.1908), channel_id=1, source_target_pairs={{64,0},{128,64},{192,128},{256,192},{320,256},{384,320},{448,384},... | collective-permute-start | bytes 393224 | tf_op jit(solution)/shard_map/while/body/eval_jaxpr/ppermute | solution.py:12
  300.6 7.4 %collective-permute-start.1 = (bf16[2,2,128,128]{3,2,1,0:T(8,128)(2,1)S(1)}, bf16[2,2,128,128]{3,2,1,0:T(8,128)(2,1)S(1)}, u32[]{:S(2)}, u32[]{:S(2)}) collective-permute-start(bf16[2,2,128,128]{3,2,1,0:T(8,128)(2,1)S(1)} %get-tuple-element.1908), channel_id=1, source_target_pairs={{64,0},{128,64},{192,128},{256,192},{320,256},{384,320},{448,384},... | collective-permute-start | bytes 393224 | tf_op jit(solution)/shard_map/while/body/eval_jaxpr/ppermute | solution.py:12
  308.8 11.8 %collective-permute-start.1 = (bf16[2,2,128,128]{3,2,1,0:T(8,128)(2,1)S(1)}, bf16[2,2,128,128]{3,2,1,0:T(8,128)(2,1)S(1)}, u32[]{:S(2)}, u32[]{:S(2)}) collective-permute-start(bf16[2,2,128,128]{3,2,1,0:T(8,128)(2,1)S(1)} %get-tuple-element.1908), channel_id=1, source_target_pairs={{64,0},{128,64},{192,128},{256,192},{320,256},{384,320},{448,384},... | collective-permute-start | bytes 393224 | tf_op jit(solution)/shard_map/while/body/eval_jaxpr/ppermute | solution.py:12
  321.5 7.4 %collective-permute-start.1 = (bf16[2,2,128,128]{3,2,1,0:T(8,128)(2,1)S(1)}, bf16[2,2,128,128]{3,2,1,0:T(8,128)(2,1)S(1)}, u32[]{:S(2)}, u32[]{:S(2)}) collective-permute-start(bf16[2,2,128,128]{3,2,1,0:T(8,128)(2,1)S(1)} %get-tuple-element.1908), channel_id=1, source_target_pairs={{64,0},{128,64},{192,128},{256,192},{320,256},{384,320},{448,384},... | collective-permute-start | bytes 393224 | tf_op jit(solution)/shard_map/while/body/eval_jaxpr/ppermute | solution.py:12
  329.7 8.2 %collective-permute-start.1 = (bf16[2,2,128,128]{3,2,1,0:T(8,128)(2,1)S(1)}, bf16[2,2,128,128]{3,2,1,0:T(8,128)(2,1)S(1)}, u32[]{:S(2)}, u32[]{:S(2)}) collective-permute-start(bf16[2,2,128,128]{3,2,1,0:T(8,128)(2,1)S(1)} %get-tuple-element.1908), channel_id=1, source_target_pairs={{64,0},{128,64},{192,128},{256,192},{320,256},{384,320},{448,384},... | collective-permute-start | bytes 393224 | tf_op jit(solution)/shard_map/while/body/eval_jaxpr/ppermute | solution.py:12
  338.8 7.4 %collective-permute-start.1 = (bf16[2,2,128,128]{3,2,1,0:T(8,128)(2,1)S(1)}, bf16[2,2,128,128]{3,2,1,0:T(8,128)(2,1)S(1)}, u32[]{:S(2)}, u32[]{:S(2)}) collective-permute-start(bf16[2,2,128,128]{3,2,1,0:T(8,128)(2,1)S(1)} %get-tuple-element.1908), channel_id=1, source_target_pairs={{64,0},{128,64},{192,128},{256,192},{320,256},{384,320},{448,384},... | collective-permute-start | bytes 393224 | tf_op jit(solution)/shard_map/while/body/eval_jaxpr/ppermute | solution.py:12
  347.0 11.8 %collective-permute-start.1 = (bf16[2,2,128,128]{3,2,1,0:T(8,128)(2,1)S(1)}, bf16[2,2,128,128]{3,2,1,0:T(8,128)(2,1)S(1)}, u32[]{:S(2)}, u32[]{:S(2)}) collective-permute-start(bf16[2,2,128,128]{3,2,1,0:T(8,128)(2,1)S(1)} %get-tuple-element.1908), channel_id=1, source_target_pairs={{64,0},{128,64},{192,128},{256,192},{320,256},{384,320},{448,384},... | collective-permute-start | bytes 393224 | tf_op jit(solution)/shard_map/while/body/eval_jaxpr/ppermute | solution.py:12
  359.7 7.5 %collective-permute-start.1 = (bf16[2,2,128,128]{3,2,1,0:T(8,128)(2,1)S(1)}, bf16[2,2,128,128]{3,2,1,0:T(8,128)(2,1)S(1)}, u32[]{:S(2)}, u32[]{:S(2)}) collective-permute-start(bf16[2,2,128,128]{3,2,1,0:T(8,128)(2,1)S(1)} %get-tuple-element.1908), channel_id=1, source_target_pairs={{64,0},{128,64},{192,128},{256,192},{320,256},{384,320},{448,384},... | collective-permute-start | bytes 393224 | tf_op jit(solution)/shard_map/while/body/eval_jaxpr/ppermute | solution.py:12
  368.0 7.9 %collective-permute-start.1 = (bf16[2,2,128,128]{3,2,1,0:T(8,128)(2,1)S(1)}, bf16[2,2,128,128]{3,2,1,0:T(8,128)(2,1)S(1)}, u32[]{:S(2)}, u32[]{:S(2)}) collective-permute-start(bf16[2,2,128,128]{3,2,1,0:T(8,128)(2,1)S(1)} %get-tuple-element.1908), channel_id=1, source_target_pairs={{64,0},{128,64},{192,128},{256,192},{320,256},{384,320},{448,384},... | collective-permute-start | bytes 393224 | tf_op jit(solution)/shard_map/while/body/eval_jaxpr/ppermute | solution.py:12
  376.7 7.5 %collective-permute-start.1 = (bf16[2,2,128,128]{3,2,1,0:T(8,128)(2,1)S(1)}, bf16[2,2,128,128]{3,2,1,0:T(8,128)(2,1)S(1)}, u32[]{:S(2)}, u32[]{:S(2)}) collective-permute-start(bf16[2,2,128,128]{3,2,1,0:T(8,128)(2,1)S(1)} %get-tuple-element.1908), channel_id=1, source_target_pairs={{64,0},{128,64},{192,128},{256,192},{320,256},{384,320},{448,384},... | collective-permute-start | bytes 393224 | tf_op jit(solution)/shard_map/while/body/eval_jaxpr/ppermute | solution.py:12
  385.1 11.9 %collective-permute-start.1 = (bf16[2,2,128,128]{3,2,1,0:T(8,128)(2,1)S(1)}, bf16[2,2,128,128]{3,2,1,0:T(8,128)(2,1)S(1)}, u32[]{:S(2)}, u32[]{:S(2)}) collective-permute-start(bf16[2,2,128,128]{3,2,1,0:T(8,128)(2,1)S(1)} %get-tuple-element.1908), channel_id=1, source_target_pairs={{64,0},{128,64},{192,128},{256,192},{320,256},{384,320},{448,384},... | collective-permute-start | bytes 393224 | tf_op jit(solution)/shard_map/while/body/eval_jaxpr/ppermute | solution.py:12
  397.8 7.5 %collective-permute-start.1 = (bf16[2,2,128,128]{3,2,1,0:T(8,128)(2,1)S(1)}, bf16[2,2,128,128]{3,2,1,0:T(8,128)(2,1)S(1)}, u32[]{:S(2)}, u32[]{:S(2)}) collective-permute-start(bf16[2,2,128,128]{3,2,1,0:T(8,128)(2,1)S(1)} %get-tuple-element.1908), channel_id=1, source_target_pairs={{64,0},{128,64},{192,128},{256,192},{320,256},{384,320},{448,384},... | collective-permute-start | bytes 393224 | tf_op jit(solution)/shard_map/while/body/eval_jaxpr/ppermute | solution.py:12
  406.2 7.9 %collective-permute-start.1 = (bf16[2,2,128,128]{3,2,1,0:T(8,128)(2,1)S(1)}, bf16[2,2,128,128]{3,2,1,0:T(8,128)(2,1)S(1)}, u32[]{:S(2)}, u32[]{:S(2)}) collective-permute-start(bf16[2,2,128,128]{3,2,1,0:T(8,128)(2,1)S(1)} %get-tuple-element.1908), channel_id=1, source_target_pairs={{64,0},{128,64},{192,128},{256,192},{320,256},{384,320},{448,384},... | collective-permute-start | bytes 393224 | tf_op jit(solution)/shard_map/while/body/eval_jaxpr/ppermute | solution.py:12
  414.9 160.4 %collective-permute-start.1 = (bf16[2,2,128,128]{3,2,1,0:T(8,128)(2,1)S(1)}, bf16[2,2,128,128]{3,2,1,0:T(8,128)(2,1)S(1)}, u32[]{:S(2)}, u32[]{:S(2)}) collective-permute-start(bf16[2,2,128,128]{3,2,1,0:T(8,128)(2,1)S(1)} %get-tuple-element.1908), channel_id=1, source_target_pairs={{64,0},{128,64},{192,128},{256,192},{320,256},{384,320},{448,384},... | collective-permute-start | bytes 393224 | tf_op jit(solution)/shard_map/while/body/eval_jaxpr/ppermute | solution.py:12
  584.7 7.8 %collective-permute-start.1 = (bf16[2,2,128,128]{3,2,1,0:T(8,128)(2,1)S(1)}, bf16[2,2,128,128]{3,2,1,0:T(8,128)(2,1)S(1)}, u32[]{:S(2)}, u32[]{:S(2)}) collective-permute-start(bf16[2,2,128,128]{3,2,1,0:T(8,128)(2,1)S(1)} %get-tuple-element.1908), channel_id=1, source_target_pairs={{64,0},{128,64},{192,128},{256,192},{320,256},{384,320},{448,384},... | collective-permute-start | bytes 393224 | tf_op jit(solution)/shard_map/while/body/eval_jaxpr/ppermute | solution.py:12
  602.0 7.4 %collective-permute-start.1 = (bf16[2,2,128,128]{3,2,1,0:T(8,128)(2,1)S(1)}, bf16[2,2,128,128]{3,2,1,0:T(8,128)(2,1)S(1)}, u32[]{:S(2)}, u32[]{:S(2)}) collective-permute-start(bf16[2,2,128,128]{3,2,1,0:T(8,128)(2,1)S(1)} %get-tuple-element.1908), channel_id=1, source_target_pairs={{64,0},{128,64},{192,128},{256,192},{320,256},{384,320},{448,384},... | collective-permute-start | bytes 393224 | tf_op jit(solution)/shard_map/while/body/eval_jaxpr/ppermute | solution.py:12
  619.0 7.4 %collective-permute-start.1 = (bf16[2,2,128,128]{3,2,1,0:T(8,128)(2,1)S(1)}, bf16[2,2,128,128]{3,2,1,0:T(8,128)(2,1)S(1)}, u32[]{:S(2)}, u32[]{:S(2)}) collective-permute-start(bf16[2,2,128,128]{3,2,1,0:T(8,128)(2,1)S(1)} %get-tuple-element.1908), channel_id=1, source_target_pairs={{64,0},{128,64},{192,128},{256,192},{320,256},{384,320},{448,384},... | collective-permute-start | bytes 393224 | tf_op jit(solution)/shard_map/while/body/eval_jaxpr/ppermute | solution.py:12
  635.8 3.2 collective-permute-start.1
  660.0 7.4 %collective-permute-start.3 = (bf16[2,1,128,256]{3,2,1,0:T(8,128)(2,1)S(1)}, bf16[2,1,128,256]{3,2,1,0:T(8,128)(2,1)S(1)}, u32[]{:S(2)}, u32[]{:S(2)}) collective-permute-start(bf16[2,1,128,256]{3,2,1,0:T(8,128)(2,1)S(1)} %slice.228), channel_id=1, source_target_pairs={{0,1},{1,2},{2,3},{3,4},{4,5},{5,6},{6,7},{7,8},{8,9},{9,10},{10,1... | collective-permute-start | bytes 393224 | tf_op jit(solution)/shard_map/ppermute | solution.py:12
where the time goes:
time: 671 us; the launch traced here: 668 us
  waiting for transfers between devices  305 us (45%)
  starting transfers between devices  181 us (27%)
  matrix products  52.9 us (8%)
  local copies, waits for them, and re-layouts  50.6 us (8%)
  between operations  30.5 us (5%)
  loops' own time  29.1 us (4%)
  other arithmetic  19.7 us (3%)
    ppermute x40, waiting for transfers between devices, shifted_2(): return lax.ppermute(value, axis, pairs)  305 us
    ppermute x40, starting transfers between devices, shifted_2(): return lax.ppermute(value, axis, pairs)  181 us
    dot_general x64, matrix products, right_product(): jnp.einsum('...mn,nk->...mk', field, matrix, precision=lax.Precision.HIGH...  31.3 us
    dot_general x64, matrix products, left_product(): jnp.einsum('mn,...nk->...mk', matrix, field, precision=lax.Precision.HIGH...  21.6 us
    dynamic_update_slice x8, local copies, waits for them, and re-layouts, on_device(): grad_ext = lax.dynamic_update_slice(grad_ext, current + piece, place)  17.7 us
    gather x24, local copies, waits for them, and re-layouts  15.9 us
  transfers between devices with their start and end apart: 40, of which 39 were waited for; matrix products, arithmetic and copies ran while one was open for 0% of the time, Pallas kernels for 0%

commit v1 on v0

v1 whole, which is shorter than its diff:
```python
import functools
import math

import jax
import jax.numpy as jnp
import numpy as np
from jax import lax
from jax.experimental import pallas as pl
from jax.experimental.pallas import tpu as pltpu
from jax.sharding import PartitionSpec as P

MESH = pl.DeviceIdType.MESH
BF16 = jnp.bfloat16
F32 = jnp.float32


def host_tables(order):
    index = np.arange(order)
    dft = np.exp(-2j * np.pi * (np.outer(index, index) % order) / order) / math.sqrt(order)
    shifted = (index + order // 2) % order - order // 2
    phase = np.exp(-1j * np.pi * (shifted * shifted) / (2 * order))
    step = dft.conj() @ (phase[:, None] * dft)

    def halves(matrix):
        right = np.block([[matrix.real, matrix.imag], [-matrix.imag, matrix.real]])
        left = np.block([[matrix.real, -matrix.imag], [matrix.imag, matrix.real]])
        parts = []
        for form in (right, left):
            high = form.astype(np.float32).astype(jnp.bfloat16)
            low = (form - high.astype(np.float64)).astype(np.float32).astype(jnp.bfloat16)
            parts += [high, low]
        return np.stack(parts)

    return halves(step), halves(dft)


def dot(a, b):
    return jnp.dot(a, b, preferred_element_type=F32)


def split(value):
    high = value.astype(BF16)
    return high, (value - high.astype(F32)).astype(BF16)


def sandwich(re, im, tab):
    n = re.shape[0]
    high, low = split(jnp.concatenate([re, im], axis=1))
    half = dot(high, tab[0]) + dot(low, tab[0]) + dot(high, tab[1])
    high, low = split(jnp.concatenate([half[:, :n], half[:, n:]], axis=0))
    full = dot(tab[2], high) + dot(tab[2], low) + dot(tab[3], high)
    return full[:n], full[n:]


def picks(shape, start, along):
    a = lax.broadcasted_iota(jnp.int32, shape, along)
    b = lax.broadcasted_iota(jnp.int32, shape, 1 - along)
    return jnp.where(a == b + start, 1.0, 0.0).astype(BF16)


def kernel(
    ox_ref,
    oy_ref,
    count_ref,
    contrast_ref,
    probe_ref,
    measured_ref,
    step_ref,
    dft_ref,
    out_ref,
    ext,
    blocks,
    trans,
    waves,
    sent,
    landed,
    spread,
    rim_out,
    rim_in,
    block_send,
    block_recv,
    grad_send,
    grad_recv,
    rim_send,
    rim_recv,
    *,
    n_beam,
    n_lat,
):
    slots, n = measured_ref.shape[0], measured_ref.shape[1]
    wide = contrast_ref.shape[3]
    stride = n_beam // slots
    me = lax.axis_index("beam")
    lat = lax.axis_index("lat")
    before = lax.rem(lat + n_lat - 1, n_lat)
    after = lax.rem(lat + 1, n_lat)
    works = lax.rem(me, stride) == 0
    slot = me // stride

    barrier = pltpu.get_barrier_semaphore()
    for other in (before, after):
        pl.semaphore_signal(barrier, inc=1, device_id={"lat": other}, device_id_type=MESH)

    @pl.loop(1, n_beam)
    def _(d):
        other = lax.rem(me + d, n_beam)
        pl.semaphore_signal(barrier, inc=1, device_id={"beam": other}, device_id_type=MESH)

    ext[0:n, 0:wide] = contrast_ref[0, 0].astype(BF16)
    ext[0:n, wide : 2 * wide] = contrast_ref[1, 0].astype(BF16)
    pl.semaphore_wait(barrier, n_beam + 1)

    rim = pltpu.make_async_remote_copy(
        src_ref=ext.at[0:n],
        dst_ref=ext.at[n : 2 * n],
        send_sem=rim_send.at[0],
        recv_sem=rim_recv.at[0],
        device_id={"lat": before},
        device_id_type=MESH,
    )
    rim.start()
    rim.wait_recv()

    def block_copy(j):
        return pltpu.make_async_remote_copy(
            src_ref=blocks.at[j],
            dst_ref=trans.at[me],
            send_sem=block_send.at[j],
            recv_sem=block_recv.at[me],
            device_id={"beam": j * stride},
            device_id_type=MESH,
        )

    @pl.loop(0, slots)
    def _(j):
        rows = picks((n, 2 * n), ox_ref[j], 1)
        columns = picks((wide, n), oy_ref[j], 0)
        beyond = lax.broadcasted_iota(jnp.int32, (n, 2 * wide), 0) + ox_ref[j] >= n
        picked = dot(rows, ext[...])
        picked = jnp.where(beyond & (lat == n_lat - 1), 0.0, picked).astype(BF16)
        blocks[j, 0] = dot(picked[:, 0:wide], columns).astype(BF16)
        blocks[j, 1] = dot(picked[:, wide : 2 * wide], columns).astype(BF16)

        @pl.when(j * stride != me)
        def _():
            block_copy(j).start()

        @pl.when(j * stride == me)
        def _():
            pltpu.make_async_copy(blocks.at[j], trans.at[me], block_recv.at[me]).start()

    def grad_copy(k):
        return pltpu.make_async_remote_copy(
            src_ref=sent.at[k],
            dst_ref=landed.at[slot],
            send_sem=grad_send.at[k],
            recv_sem=grad_recv.at[slot],
            device_id={"beam": k},
            device_id_type=MESH,
        )

    def times_trans(k, re, im):
        t_re = 1.0 + trans[k, 0].astype(F32)
        t_im = trans[k, 1].astype(F32)
        return t_re * re - t_im * im, t_re * im + t_im * re

    def wait_block(k):
        pltpu.make_async_copy(blocks.at[0], trans.at[k], block_recv.at[k]).wait()

    def give(k, d_re, d_im):
        w_re, w_im = waves[k, 0], waves[k, 1]
        sent[k, 0] = (w_re * d_re - w_im * d_im).astype(BF16)
        sent[k, 1] = -(w_re * d_im + w_im * d_re).astype(BF16)

        @pl.when(k != me)
        def _():
            grad_copy(k).start()

        @pl.when(k == me)
        def _():
            pltpu.make_async_copy(sent.at[k], landed.at[slot], grad_recv.at[slot]).start()

    @pl.when(works)
    def _():
        waves[0] = probe_ref[...]

        @pl.loop(0, n_beam - 1)
        def _(k):
            wait_block(k)
            re, im = times_trans(k, waves[k, 0], waves[k, 1])
            re, im = sandwich(re, im, step_ref)
            waves[k + 1, 0] = re
            waves[k + 1, 1] = im

        last = n_beam - 1
        wait_block(last)
        re, im = times_trans(last, waves[last, 0], waves[last, 1])
        re, im = sandwich(re, im, dft_ref)
        live = jnp.where(slot < count_ref[0], 1.0, 0.0)
        misfit = live * (re * re + im * im - measured_ref[slot])
        d_re, d_im = sandwich(misfit * re, -(misfit * im), dft_ref)
        give(last, d_re, d_im)
        re, im = times_trans(last, d_re, d_im)
        waves[last, 0] = re
        waves[last, 1] = im

        @pl.loop(0, last)
        def _(i):
            k = last - 1 - i
            d_re, d_im = sandwich(waves[last, 0], waves[last, 1], step_ref)
            give(k, d_re, d_im)
            re, im = times_trans(k, d_re, d_im)
            waves[last, 0] = re
            waves[last, 1] = im

    @pl.loop(0, slots)
    def _(j):
        pltpu.make_async_copy(sent.at[0], landed.at[j], grad_recv.at[j]).wait()
        columns = picks((n, wide), oy_ref[j], 1)
        spread[j, :, 0:wide] = dot(landed[j, 0], columns).astype(BF16)
        spread[j, :, wide : 2 * wide] = dot(landed[j, 1], columns).astype(BF16)

    def gathered(shift):
        def add(j, total):
            rows = picks((n, n), ox_ref[j] - shift, 0)
            return total + dot(rows, spread[j])

        return lax.fori_loop(0, slots, add, jnp.zeros((n, 2 * wide), F32))

    rim_out[...] = gathered(n).astype(BF16)
    back = pltpu.make_async_remote_copy(
        src_ref=rim_out,
        dst_ref=rim_in,
        send_sem=rim_send.at[1],
        recv_sem=rim_recv.at[1],
        device_id={"lat": after},
        device_id_type=MESH,
    )
    back.start()
    own = gathered(0)
    back.wait_recv()
    own = own + jnp.where(lat == 0, 0.0, rim_in[...].astype(F32))
    out_ref[0, 0] = own[:, 0:wide]
    out_ref[1, 0] = own[:, wide : 2 * wide]

    rim.wait_send()
    back.wait_send()

    @pl.loop(0, slots)
    def _(j):
        @pl.when(j * stride != me)
        def _():
            block_copy(j).wait_send()

    @pl.when(works)
    def _():
        @pl.loop(0, n_beam)
        def _(k):
            @pl.when(k != me)
            def _():
                grad_copy(k).wait_send()


def on_device(n_beam, n_lat, contrast, probe, offset_x, offset_y, probe_count, measured):
    slots, n = measured.shape[0], measured.shape[1]
    wide = contrast.shape[3]
    step, dft = host_tables(n)
    vmem = pl.BlockSpec(memory_space=pltpu.VMEM)
    smem = pl.BlockSpec(memory_space=pltpu.SMEM)
    return pl.pallas_call(
        functools.partial(kernel, n_beam=n_beam, n_lat=n_lat),
        out_shape=jax.ShapeDtypeStruct(contrast.shape, F32),
        in_specs=[smem] * 3 + [vmem] * 5,
        out_specs=vmem,
        scratch_shapes=[
            pltpu.VMEM((2 * n, 2 * wide), BF16),
            pltpu.VMEM((slots, 2, n, n), BF16),
            pltpu.VMEM((n_beam, 2, n, n), BF16),
            pltpu.VMEM((n_beam, 2, n, n), F32),
            pltpu.VMEM((n_beam, 2, n, n), BF16),
            pltpu.VMEM((slots, 2, n, n), BF16),
            pltpu.VMEM((slots, n, 2 * wide), BF16),
            pltpu.VMEM((n, 2 * wide), BF16),
            pltpu.VMEM((n, 2 * wide), BF16),
            pltpu.SemaphoreType.DMA((slots,)),
            pltpu.SemaphoreType.DMA((n_beam,)),
            pltpu.SemaphoreType.DMA((n_beam,)),
            pltpu.SemaphoreType.DMA((slots,)),
            pltpu.SemaphoreType.DMA((2,)),
            pltpu.SemaphoreType.DMA((2,)),
        ],
        compiler_params=pltpu.CompilerParams(
            collective_id=0, has_side_effects=True, vmem_limit_bytes=40 << 20
        ),
    )(offset_x, offset_y, probe_count, contrast, probe, measured, jnp.asarray(step), jnp.asarray(dft))


def solution(mesh):
    in_specs = (
        P(None, "beam", "lat", None),
        P(),
        P("lat"),
        P("lat"),
        P("lat"),
        P("lat", None, None),
    )
    return jax.shard_map(
        functools.partial(on_device, mesh.shape["beam"], mesh.shape["lat"]),
        mesh=mesh,
        in_specs=in_specs,
        out_specs=P(None, "beam", "lat", None),
        check_vma=False,
    )
```

time: 671 us -> 80.6 us (0.12)
  the two profiles are of different devices: /device:TPU:16 before, /device:TPU:8 now
where the time goes in v1:
time: 80.6 us; the launch traced here: 80.3 us
  Pallas kernels  73.9 us (92%)
  local copies, waits for them, and re-layouts  5.68 us (7%)
    pallas_call x1, Pallas kernels, on_device(): pl.pallas_call(functools.partial(kernel, n_beam=n_beam, n_lat=n_lat), out...  73.9 us
    unnamed x15, local copies, waits for them, and re-layouts  5.68 us

profile of v1, /device:TPU:8, one launch (start us, length us, event | category | flops | bytes accessed | tf_op | source)
XLA Modules:
  0.0 80.3 jit_solution(5337197106924926357)
XLA Ops:
  0.0 0.0 copy-start.6
  0.0 0.0 copy-start.5
  0.7 0.0 copy-done.6
  0.7 0.0 copy-done.5
  0.7 0.0 copy-start
  0.7 1.0 %copy-done = f32[8,128,128]{2,1,0:T(8,128)S(1)} copy-done((f32[8,128,128]{2,1,0:T(8,128)S(1)}, f32[8,128,128]{2,1,0:T(8,128)}, u32[]{:S(2)}) %copy-start) | copy-done | bytes 524312
  1.7 0.0 copy-start.1
  1.7 1.0 %copy-done.1 = bf16[4,256,256]{2,1,0:T(8,128)(2,1)S(1)} copy-done((bf16[4,256,256]{2,1,0:T(8,128)(2,1)S(1)}, bf16[4,256,256]{2,1,0:T(8,128)(2,1)}, u32[]{:S(2)}) %copy-start.1) | copy-done | bytes 524312
  2.8 0.0 copy-start.2
  2.8 1.0 %copy-done.2 = bf16[4,256,256]{2,1,0:T(8,128)(2,1)S(1)} copy-done((bf16[4,256,256]{2,1,0:T(8,128)(2,1)S(1)}, bf16[4,256,256]{2,1,0:T(8,128)(2,1)}, u32[]{:S(2)}) %copy-start.2) | copy-done | bytes 524312
  3.8 0.0 copy-start.3
  3.8 0.9 %copy-done.3 = f32[2,1,128,256]{3,2,1,0:T(8,128)S(1)} copy-done((f32[2,1,128,256]{3,2,1,0:T(8,128)S(1)}, f32[2,1,128,256]{3,2,1,0:T(8,128)}, u32[]{:S(2)}) %copy-start.3) | copy-done | bytes 262168
  4.8 0.0 copy-start.4
  4.8 0.9 %copy-done.4 = f32[2,128,128]{2,1,0:T(8,128)S(1)} copy-done((f32[2,128,128]{2,1,0:T(8,128)S(1)}, f32[2,128,128]{2,1,0:T(8,128)}, u32[]{:S(2)}) %copy-start.4) | copy-done | bytes 131096
  5.7 73.9 %shard_map.82 = f32[2,1,128,256]{3,2,1,0:T(8,128)S(1)} custom-call(s32[8]{0:T(128)S(1)} %copy-done.5, s32[8]{0:T(128)S(1)} %copy-done.6, s32[1]{0:T(128)S(6)} %copy.10.count_ref, f32[2,1,128,256]{3,2,1,0:T(8,128)S(1)} %copy-done.3, f32[2,128,128]{2,1,0:T(8,128)S(1)} %copy-done.4, f32[8,128,128]{2,1,0:T(8,128)S(1)} %copy-done, ...), custom_call_target="tpu_custom_call" | custom-call | tf_op jit(solution)/shard_map/pallas_call | solution.py:270
  79.6 0.7 copy.11
Async XLA Ops:
  0.0 0.7 copy-start.6
  0.0 0.7 copy-start.5
  0.7 1.0 %copy-start = (f32[8,128,128]{2,1,0:T(8,128)S(1)}, f32[8,128,128]{2,1,0:T(8,128)}, u32[]{:S(2)}) copy-start(f32[8,128,128]{2,1,0:T(8,128)} %measured_ref.1) | copy-start | bytes 1572868
  1.7 1.0 %copy-start.1 = (bf16[4,256,256]{2,1,0:T(8,128)(2,1)S(1)}, bf16[4,256,256]{2,1,0:T(8,128)(2,1)}, u32[]{:S(2)}) copy-start(bf16[4,256,256]{2,1,0:T(8,128)(2,1)} %constant.5.clone.dft_ref) | copy-start | bytes 1572868
  2.8 1.0 %copy-start.2 = (bf16[4,256,256]{2,1,0:T(8,128)(2,1)S(1)}, bf16[4,256,256]{2,1,0:T(8,128)(2,1)}, u32[]{:S(2)}) copy-start(bf16[4,256,256]{2,1,0:T(8,128)(2,1)} %constant.4.clone.step_ref) | copy-start | bytes 1572868
  3.8 0.9 %copy-start.3 = (f32[2,1,128,256]{3,2,1,0:T(8,128)S(1)}, f32[2,1,128,256]{3,2,1,0:T(8,128)}, u32[]{:S(2)}) copy-start(f32[2,1,128,256]{3,2,1,0:T(8,128)} %contrast_ref.1) | copy-start | bytes 786436
  4.8 0.9 %copy-start.4 = (f32[2,128,128]{2,1,0:T(8,128)S(1)}, f32[2,128,128]{2,1,0:T(8,128)}, u32[]{:S(2)}) copy-start(f32[2,128,128]{2,1,0:T(8,128)} %probe_ref.1) | copy-start | bytes 393220

commit v2 on v1

v2 whole, which is shorter than its diff:
```python
import functools
import math

import jax
import jax.numpy as jnp
import numpy as np
from jax import lax
from jax.experimental import pallas as pl
from jax.experimental.pallas import tpu as pltpu
from jax.sharding import PartitionSpec as P

MESH = pl.DeviceIdType.MESH
BF16 = jnp.bfloat16
F32 = jnp.float32
ROW_BLOCKS = 2


def host_tables(order):
    index = np.arange(order)
    dft = np.exp(-2j * np.pi * (np.outer(index, index) % order) / order) / math.sqrt(order)
    shifted = (index + order // 2) % order - order // 2
    phase = np.exp(-1j * np.pi * (shifted * shifted) / (2 * order))
    step = dft.conj() @ (phase[:, None] * dft)

    def halves(form):
        high = form.astype(np.float32).astype(jnp.bfloat16)
        low = (form - high.astype(np.float64)).astype(np.float32).astype(jnp.bfloat16)
        return np.stack([high, low])

    rights, lefts = [], []
    for matrix in (step, dft):
        re, im = matrix.real, matrix.imag
        rights.append(halves(np.block([[re, im], [-im, re]])))
        rows = np.block([[re, -im], [im, re]]).reshape(2, ROW_BLOCKS, order // ROW_BLOCKS, 2 * order)
        lefts.append(halves(rows.transpose(1, 0, 2, 3).reshape(2 * order, 2 * order)))
    return np.stack(rights), np.stack(lefts)


def dot(a, b):
    return jnp.dot(a, b, preferred_element_type=F32)


def by_right(blocks, right):
    re, im = [], []
    for block_re, block_im in blocks:
        n = block_re.shape[1]
        both = jnp.concatenate([block_re, block_im], axis=1).astype(BF16)
        half = dot(both, right[0]) + dot(both, right[1])
        re.append(half[:, :n].astype(BF16))
        im.append(half[:, n:].astype(BF16))
    return jnp.concatenate(re + im, axis=0)


def by_left(left, half):
    blocks = []
    n = left.shape[1] // (2 * ROW_BLOCKS)
    for b in range(ROW_BLOCKS):
        rows = slice(2 * b * n, 2 * (b + 1) * n)
        both = dot(left[0, rows], half) + dot(left[1, rows], half)
        blocks.append((both[:n], both[n:]))
    return blocks


def picks(shape, start, along):
    a = lax.broadcasted_iota(jnp.int32, shape, along)
    b = lax.broadcasted_iota(jnp.int32, shape, 1 - along)
    return jnp.where(a == b + start, 1.0, 0.0).astype(BF16)


def kernel(
    ox_ref,
    oy_ref,
    count_ref,
    contrast_hbm,
    probe_hbm,
    measured_hbm,
    rights_hbm,
    lefts_hbm,
    out_hbm,
    contrast,
    measured,
    rights,
    lefts,
    ext,
    cut_rows,
    cut_columns,
    put_columns,
    put_rows,
    blocks,
    trans,
    waves,
    half,
    sent,
    landed,
    spread,
    rim_out,
    rim_in,
    out,
    load,
    store,
    block_send,
    block_recv,
    grad_send,
    grad_recv,
    rim_send,
    rim_recv,
    back_send,
    back_recv,
    here,
    *,
    n_beam,
    n_lat,
):
    slots, n = measured_hbm.shape[0], measured_hbm.shape[1]
    wide = contrast_hbm.shape[3]
    stride = n_beam // slots
    me = lax.axis_index("beam")
    lat = lax.axis_index("lat")
    before, after = lat - 1, lat + 1
    has_before, has_after = lat > 0, lat < n_lat - 1

    def hosts(i):
        return lax.rem(i, stride) == 0

    def slot_of(i):
        return i // stride

    def host(j):
        return j * stride

    lower = jnp.where(hosts(me), me, (me + stride - 1) // stride)
    works = hosts(me)
    slot = slot_of(me)

    def meets(i, j):
        return hosts(i) | hosts(j)

    object_load = pltpu.make_async_copy(contrast_hbm, contrast, load.at[0])
    object_load.start()
    loads = [
        pltpu.make_async_copy(probe_hbm, waves.at[0], load.at[1]),
        pltpu.make_async_copy(rights_hbm, rights, load.at[2]),
        pltpu.make_async_copy(lefts_hbm, lefts, load.at[3]),
        pltpu.make_async_copy(measured_hbm.at[slot], measured, load.at[4]),
    ]

    barrier = pltpu.get_barrier_semaphore()
    for there, other in ((has_before, before), (has_after, after)):

        @pl.when(there)
        def _(other=other):
            pl.semaphore_signal(barrier, inc=1, device_id={"lat": other}, device_id_type=MESH)

    @pl.loop(me + 1, n_beam)
    def _(other):
        @pl.when(meets(me, other))
        def _():
            pl.semaphore_signal(barrier, inc=1, device_id={"beam": other}, device_id_type=MESH)

    object_load.wait()
    for part in (0, 1):
        ext[part, 0:n] = contrast[part, 0].astype(BF16)
    pl.semaphore_wait(barrier, lower + jnp.where(has_before & has_after, 2, 1))

    rims = [
        pltpu.make_async_remote_copy(
            src_ref=ext.at[part, 0:n],
            dst_ref=ext.at[part, n : 2 * n],
            send_sem=rim_send.at[part],
            recv_sem=rim_recv.at[part],
            device_id={"lat": before},
            device_id_type=MESH,
        )
        for part in (0, 1)
    ]

    @pl.when(has_before)
    def _():
        for rim in rims:
            rim.start()

    @pl.loop(0, me)
    def _(other):
        @pl.when(meets(me, other))
        def _():
            pl.semaphore_signal(here.at[me], inc=1, device_id={"beam": other}, device_id_type=MESH)

    @pl.when(works)
    def _():
        for copy in loads:
            copy.start()

    @pl.loop(0, slots)
    def _(j):
        x, y = ox_ref[j], oy_ref[j]
        cut_rows[j] = picks((n, 2 * n), x, 1)
        cut_columns[j] = picks((wide, n), y, 0)
        put_columns[j] = picks((n, wide), y, 1)
        put_rows[j, 0] = picks((n, n), x, 0)
        put_rows[j, 1] = picks((n, n), x - n, 0)

    def block_copy(j):
        return pltpu.make_async_remote_copy(
            src_ref=blocks.at[j],
            dst_ref=trans.at[me],
            send_sem=block_send.at[j],
            recv_sem=block_recv.at[me],
            device_id={"beam": host(j)},
            device_id_type=MESH,
        )

    group = 4
    for part in (0, 1):

        @pl.when(has_after)
        def _(part=part):
            rims[part].wait_recv()

        @pl.when(jnp.logical_not(has_after))
        def _(part=part):
            ext[part, n : 2 * n] = jnp.zeros((n, wide), BF16)

        @pl.loop(0, slots // group)
        def _(g, part=part):
            members = [g * group + m for m in range(group)]
            picked = [dot(cut_rows[j], ext[part]).astype(BF16) for j in members]
            picked = [dot(p, cut_columns[j]).astype(BF16) for p, j in zip(picked, members)]
            for p, j in zip(picked, members):
                blocks[j, part] = p
            if part == 1:
                for j in members:

                    @pl.when(host(j) < me)
                    def _(j=j):
                        block_copy(j).start()

                    @pl.when(host(j) == me)
                    def _(j=j):
                        pltpu.make_async_copy(blocks.at[j], trans.at[me], block_recv.at[me]).start()

    @pl.loop(me + 1, n_beam)
    def _(other):
        @pl.when(meets(me, other))
        def _():
            pl.semaphore_wait(here.at[other], 1)

            @pl.when(hosts(other))
            def _():
                block_copy(slot_of(other)).start()

    def grad_copy(k):
        return pltpu.make_async_remote_copy(
            src_ref=sent.at[k],
            dst_ref=landed.at[slot],
            send_sem=grad_send.at[k],
            recv_sem=grad_recv.at[slot],
            device_id={"beam": k},
            device_id_type=MESH,
        )

    tall = n // ROW_BLOCKS

    def times_trans(k, field):
        out = []
        for b, (re, im) in enumerate(field):
            rows = slice(b * tall, (b + 1) * tall)
            t_re = 1.0 + trans[k, 0, rows].astype(F32)
            t_im = trans[k, 1, rows].astype(F32)
            out.append((t_re * re - t_im * im, t_re * im + t_im * re))
        return out

    def wait_block(k):
        pltpu.make_async_copy(blocks.at[0], trans.at[k], block_recv.at[k]).wait()

    def keep(k, field):
        for b, (re, im) in enumerate(field):
            rows = slice(b * tall, (b + 1) * tall)
            waves[k, 0, rows] = re
            waves[k, 1, rows] = im

    def kept(k):
        return [
            (waves[k, 0, b * tall : (b + 1) * tall], waves[k, 1, b * tall : (b + 1) * tall])
            for b in range(ROW_BLOCKS)
        ]

    def give(k, field):
        for b, ((w_re, w_im), (d_re, d_im)) in enumerate(zip(kept(k), field)):
            rows = slice(b * tall, (b + 1) * tall)
            sent[k, 0, rows] = (w_re * d_re - w_im * d_im).astype(BF16)
            sent[k, 1, rows] = -(w_re * d_im + w_im * d_re).astype(BF16)

    def post(k):
        @pl.when(k != me)
        def _():
            grad_copy(k).start()

        @pl.when(k == me)
        def _():
            pltpu.make_async_copy(sent.at[k], landed.at[slot], grad_recv.at[slot]).start()

    @pl.when(works)
    def _():
        for copy in loads:
            copy.wait()
        wait_block(0)
        half[...] = by_right(times_trans(0, kept(0)), rights.at[0])

        @pl.loop(1, n_beam)
        def _(k):
            wait_block(k)
            field = by_left(lefts.at[0], half[...])
            keep(k, field)
            table = k // (n_beam - 1)
            half[...] = by_right(times_trans(k, field), rights.at[table])

        last = n_beam - 1
        live = jnp.where(slot < count_ref[0], 1.0, 0.0)
        field = []
        for b, (re, im) in enumerate(by_left(lefts.at[1], half[...])):
            misfit = live * (re * re + im * im - measured[b * tall : (b + 1) * tall])
            field.append((misfit * re, -(misfit * im)))
        half[...] = by_right(field, rights.at[1])

        @pl.loop(0, last)
        def _(i):
            k = last - i
            field = by_left(lefts.at[(k + 1) // n_beam], half[...])
            half[...] = by_right(times_trans(k, field), rights.at[0])
            give(k, field)
            post(k)

        give(0, by_left(lefts.at[0], half[...]))
        post(0)

    @pl.loop(0, slots)
    def _(j):
        pltpu.make_async_copy(sent.at[0], landed.at[j], grad_recv.at[j]).wait()
        both = jnp.concatenate([landed[j, 0], landed[j, 1]], axis=0)
        both = dot(both, put_columns[j]).astype(BF16)
        place = pl.ds(pl.multiple_of(j * n, n), n)
        spread[0, place] = both[0:n]
        spread[1, place] = both[n : 2 * n]

    def gathered(part, beyond):
        rows = jnp.concatenate([put_rows[j, beyond] for j in range(slots)], axis=1)
        return dot(rows, spread[part])

    backs = [
        pltpu.make_async_remote_copy(
            src_ref=rim_out.at[part],
            dst_ref=rim_in.at[part],
            send_sem=back_send.at[part],
            recv_sem=back_recv.at[part],
            device_id={"lat": after},
            device_id_type=MESH,
        )
        for part in (0, 1)
    ]
    for part in (0, 1):
        rim_out[part] = gathered(part, 1).astype(BF16)

        @pl.when(has_after)
        def _(part=part):
            backs[part].start()

    for part in (0, 1):
        out[part, 0] = gathered(part, 0)

    for part in (0, 1):

        @pl.when(has_before)
        def _(part=part):
            backs[part].wait_recv()
            out[part, 0] += rim_in[part].astype(F32)

        pltpu.make_async_copy(out.at[part], out_hbm.at[part], store.at[part]).start()

    for part in (0, 1):
        pltpu.make_async_copy(out.at[part], out_hbm.at[part], store.at[part]).wait()

        @pl.when(has_before)
        def _(part=part):
            rims[part].wait_send()

        @pl.when(has_after)
        def _(part=part):
            backs[part].wait_send()

    @pl.loop(0, slots)
    def _(j):
        @pl.when(host(j) != me)
        def _():
            block_copy(j).wait_send()

    @pl.when(works)
    def _():
        @pl.loop(0, n_beam)
        def _(k):
            @pl.when(k != me)
            def _():
                grad_copy(k).wait_send()


def on_device(n_beam, n_lat, contrast, probe, offset_x, offset_y, probe_count, measured):
    slots, n = measured.shape[0], measured.shape[1]
    wide = contrast.shape[3]
    rights, lefts = host_tables(n)
    smem = pl.BlockSpec(memory_space=pltpu.SMEM)
    hbm = pl.BlockSpec(memory_space=pltpu.HBM)
    dma = pltpu.SemaphoreType.DMA
    return pl.pallas_call(
        functools.partial(kernel, n_beam=n_beam, n_lat=n_lat),
        out_shape=jax.ShapeDtypeStruct(contrast.shape, F32),
        in_specs=[smem] * 3 + [hbm] * 5,
        out_specs=hbm,
        scratch_shapes=[
            pltpu.VMEM(contrast.shape, F32),
            pltpu.VMEM((n, n), F32),
            pltpu.VMEM(rights.shape, BF16),
            pltpu.VMEM(lefts.shape, BF16),
            pltpu.VMEM((2, 2 * n, wide), BF16),
            pltpu.VMEM((slots, n, 2 * n), BF16),
            pltpu.VMEM((slots, wide, n), BF16),
            pltpu.VMEM((slots, n, wide), BF16),
            pltpu.VMEM((slots, 2, n, n), BF16),
            pltpu.VMEM((slots, 2, n, n), BF16),
            pltpu.VMEM((n_beam, 2, n, n), BF16),
            pltpu.VMEM((n_beam, 2, n, n), F32),
            pltpu.VMEM((2 * n, n), BF16),
            pltpu.VMEM((n_beam, 2, n, n), BF16),
            pltpu.VMEM((slots, 2, n, n), BF16),
            pltpu.VMEM((2, slots * n, wide), BF16),
            pltpu.VMEM((2, n, wide), BF16),
            pltpu.VMEM((2, n, wide), BF16),
            pltpu.VMEM(contrast.shape, F32),
            dma((5,)),
            dma((2,)),
            dma((slots,)),
            dma((n_beam,)),
            dma((n_beam,)),
            dma((slots,)),
            dma((2,)),
            dma((2,)),
            dma((2,)),
            dma((2,)),
            pltpu.SemaphoreType.REGULAR((n_beam,)),
        ],
        compiler_params=pltpu.CompilerParams(
            collective_id=0, has_side_effects=True, vmem_limit_bytes=60 << 20
        ),
    )(offset_x, offset_y, probe_count, contrast, probe, measured, jnp.asarray(rights), jnp.asarray(lefts))


def solution(mesh):
    in_specs = (
        P(None, "beam", "lat", None),
        P(),
        P("lat"),
        P("lat"),
        P("lat"),
        P("lat", None, None),
    )
    return jax.shard_map(
        functools.partial(on_device, mesh.shape["beam"], mesh.shape["lat"]),
        mesh=mesh,
        in_specs=in_specs,
        out_specs=P(None, "beam", "lat", None),
        check_vma=False,
    )
```

time: 80.6 us -> 67.8 us (0.84)
  the two profiles are of different devices: /device:TPU:8 before, /device:TPU:10 now
where the time goes in v2:
time: 67.8 us; the launch traced here: 67.5 us
  Pallas kernels  65.2 us (96%)
  local copies, waits for them, and re-layouts  1.67 us (2%)
    pallas_call x1, Pallas kernels, on_device(): pl.pallas_call(functools.partial(kernel, n_beam=n_beam, n_lat=n_lat), out...  65.2 us
    unnamed x1, local copies, waits for them, and re-layouts  1.67 us

profile of v2, /device:TPU:10, one launch (start us, length us, event | category | flops | bytes accessed | tf_op | source)
XLA Modules:
  0.0 67.5 jit_solution(11679276774734950096)
XLA Ops:
  0.7 65.2 %shard_map.82 = f32[2,1,128,256]{3,2,1,0:T(8,128)} custom-call(s32[8]{0:T(128)} %ox_ref.1, s32[8]{0:T(128)} %oy_ref.1, s32[1]{0:T(128)S(6)} %copy.10.count_ref, f32[2,1,128,256]{3,2,1,0:T(8,128)} %contrast_hbm.1, f32[2,128,128]{2,1,0:T(8,128)} %probe_hbm.1, f32[8,128,128]{2,1,0:T(8,128)} %measured_hbm.1, bf16[2,2,256,256]{3,2,1,0:T(8,128)(2,1)} %constant.4.clone.rights_hbm, ...), custom_call_target="tpu_custom_call" | custom-call | tf_op jit(solution)/shard_map/pallas_call | solution.py:412
  65.9 1.7 %copy.11 = f32[2,1,128,256]{3,2,1,0:T(8,128)} copy(f32[2,1,128,256]{3,2,1,0:T(8,128)} %shard_map.82) | data formatting | bytes 524288

commit v3 on v2

--- a/solution.py
+++ b/solution.py
@@ -31,8 +31,8 @@
     for matrix in (step, dft):
         re, im = matrix.real, matrix.imag
         rights.append(halves(np.block([[re, im], [-im, re]])))
-        rows = np.block([[re, -im], [im, re]]).reshape(2, ROW_BLOCKS, order // ROW_BLOCKS, 2 * order)
-        lefts.append(halves(rows.transpose(1, 0, 2, 3).reshape(2 * order, 2 * order)))
+        rows = halves(np.block([re, im])).reshape(2, ROW_BLOCKS, order // ROW_BLOCKS, 2 * order)
+        lefts.append(rows.transpose(1, 0, 2, 3).reshape(2 * order, 2 * order))
     return np.stack(rights), np.stack(lefts)
 
 
@@ -41,23 +41,24 @@
 
 
 def by_right(blocks, right):
-    re, im = [], []
-    for block_re, block_im in blocks:
-        n = block_re.shape[1]
-        both = jnp.concatenate([block_re, block_im], axis=1).astype(BF16)
-        half = dot(both, right[0]) + dot(both, right[1])
-        re.append(half[:, :n].astype(BF16))
-        im.append(half[:, n:].astype(BF16))
-    return jnp.concatenate(re + im, axis=0)
+    halves = []
+    for re, im in blocks:
+        both = jnp.concatenate([re, im], axis=1).astype(BF16)
+        halves.append(dot(both, right[0]) + dot(both, right[1]))
+    half = jnp.concatenate(halves, axis=0)
+    n = half.shape[0]
+    turned = jnp.concatenate([-half[:, n:], half[:, :n]], axis=1)
+    return jnp.concatenate([half.astype(BF16), turned.astype(BF16)], axis=0)
 
 
 def by_left(left, half):
     blocks = []
-    n = left.shape[1] // (2 * ROW_BLOCKS)
+    n = left.shape[1] // 2
+    tall = n // ROW_BLOCKS
     for b in range(ROW_BLOCKS):
-        rows = slice(2 * b * n, 2 * (b + 1) * n)
-        both = dot(left[0, rows], half) + dot(left[1, rows], half)
-        blocks.append((both[:n], both[n:]))
+        both = dot(left[2 * b * tall : 2 * (b + 1) * tall], half)
+        both = both[:tall] + both[tall:]
+        blocks.append((both[:, :n], both[:, n:]))
     return blocks
 
 
@@ -76,7 +77,8 @@
     measured_hbm,
     rights_hbm,
     lefts_hbm,
-    out_hbm,
+    own_hbm,
+    rim_hbm,
     contrast,
     measured,
     rights,
@@ -94,7 +96,6 @@
     landed,
     spread,
     rim_out,
-    rim_in,
     out,
     load,
     store,
@@ -349,7 +350,7 @@
     backs = [
         pltpu.make_async_remote_copy(
             src_ref=rim_out.at[part],
-            dst_ref=rim_in.at[part],
+            dst_ref=rim_hbm.at[part, 0],
             send_sem=back_send.at[part],
             recv_sem=back_recv.at[part],
             device_id={"lat": after},
@@ -366,18 +367,14 @@
 
     for part in (0, 1):
         out[part, 0] = gathered(part, 0)
+        pltpu.make_async_copy(out.at[part], own_hbm.at[part], store.at[part]).start()
 
     for part in (0, 1):
+        pltpu.make_async_copy(out.at[part], own_hbm.at[part], store.at[part]).wait()
 
         @pl.when(has_before)
         def _(part=part):
             backs[part].wait_recv()
-            out[part, 0] += rim_in[part].astype(F32)
-
-        pltpu.make_async_copy(out.at[part], out_hbm.at[part], store.at[part]).start()
-
-    for part in (0, 1):
-        pltpu.make_async_copy(out.at[part], out_hbm.at[part], store.at[part]).wait()
 
         @pl.when(has_before)
         def _(part=part):
@@ -409,11 +406,14 @@
     smem = pl.BlockSpec(memory_space=pltpu.SMEM)
     hbm = pl.BlockSpec(memory_space=pltpu.HBM)
     dma = pltpu.SemaphoreType.DMA
-    return pl.pallas_call(
+    own, rim = pl.pallas_call(
         functools.partial(kernel, n_beam=n_beam, n_lat=n_lat),
-        out_shape=jax.ShapeDtypeStruct(contrast.shape, F32),
+        out_shape=[
+            jax.ShapeDtypeStruct(contrast.shape, F32),
+            jax.ShapeDtypeStruct(contrast.shape, BF16),
+        ],
         in_specs=[smem] * 3 + [hbm] * 5,
-        out_specs=hbm,
+        out_specs=[hbm, hbm],
         scratch_shapes=[
             pltpu.VMEM(contrast.shape, F32),
             pltpu.VMEM((n, n), F32),
@@ -427,11 +427,10 @@
             pltpu.VMEM((slots, 2, n, n), BF16),
             pltpu.VMEM((n_beam, 2, n, n), BF16),
             pltpu.VMEM((n_beam, 2, n, n), F32),
-            pltpu.VMEM((2 * n, n), BF16),
+            pltpu.VMEM((2 * n, 2 * n), BF16),
             pltpu.VMEM((n_beam, 2, n, n), BF16),
             pltpu.VMEM((slots, 2, n, n), BF16),
             pltpu.VMEM((2, slots * n, wide), BF16),
-            pltpu.VMEM((2, n, wide), BF16),
             pltpu.VMEM((2, n, wide), BF16),
             pltpu.VMEM(contrast.shape, F32),
             dma((5,)),
@@ -450,6 +449,7 @@
             collective_id=0, has_side_effects=True, vmem_limit_bytes=60 << 20
         ),
     )(offset_x, offset_y, probe_count, contrast, probe, measured, jnp.asarray(rights), jnp.asarray(lefts))
+    return own + jnp.where(lax.axis_index("lat") > 0, rim.astype(F32), 0.0)
 
 
 def solution(mesh):

time: 67.8 us -> 66.6 us (0.982)
  other arithmetic: 0 us -> 1.72 us
  local copies, waits for them, and re-layouts: 1.67 us -> 0 us
  Pallas kernels: 65.2 us -> 64 us
    add x0 -> x1, other arithmetic: none -> 1.72 us  [on_device(): return own + jnp.where(lax.axis_index('lat') > 0, rim.astype(F32), 0.0)]
    unnamed x1 -> x0, local copies, waits for them, and re-layouts: 1.67 us -> none
    pallas_call x1, Pallas kernels: 65.2 us -> 64 us  [on_device(): pl.pallas_call(functools.partial(kernel, n_beam=n_beam, n_lat=n_lat), out...]
where the time goes in v3:
time: 66.6 us; the launch traced here: 66.4 us
  Pallas kernels  64 us (96%)
  other arithmetic  1.72 us (3%)
    pallas_call x1, Pallas kernels, on_device(): pl.pallas_call(functools.partial(kernel, n_beam=n_beam, n_lat=n_lat), out...  64 us
    add x1, other arithmetic, on_device(): return own + jnp.where(lax.axis_index('lat') > 0, rim.astype(F32), 0.0)  1.72 us

profile of v3, /device:TPU:10, one launch (start us, length us, event | category | flops | bytes accessed | tf_op | source)
XLA Modules:
  0.0 66.4 jit_solution(3717853511848898325)
XLA Ops:
  0.7 64.0 %shard_map.82 = (f32[2,1,128,256]{3,2,1,0:T(8,128)}, bf16[2,1,128,256]{3,2,1,0:T(8,128)(2,1)}) custom-call(s32[8]{0:T(128)} %ox_ref.1, s32[8]{0:T(128)} %oy_ref.1, s32[1]{0:T(128)S(6)} %copy.9.count_ref, f32[2,1,128,256]{3,2,1,0:T(8,128)} %contrast_hbm.1, f32[2,128,128]{2,1,0:T(8,128)} %probe_hbm.1, f32[8,128,128]{2,1,0:T(8,128)} %measured_hbm.1, ...), custom_call_target="tpu_custom_call" | custom-call | tf_op jit(solution)/shard_map/pallas_call | solution.py:409
  64.7 1.7 %select_add_fusion = f32[2,1,128,256]{3,2,1,0:T(8,128)} fusion(f32[2,1,128,256]{3,2,1,0:T(8,128)} %get-tuple-element.7, bf16[2,1,128,256]{3,2,1,0:T(8,128)(2,1)} %get-tuple-element.8, pred[]{:T(512)S(6)} %gt.3), kind=kLoop, calls=%fused_computation | loop fusion | flops 196608 | bytes 655361 | tf_op jit(solution)/shard_map/add | solution.py:452

commit v4 on v3

--- a/solution.py
+++ b/solution.py
@@ -13,6 +13,7 @@
 BF16 = jnp.bfloat16
 F32 = jnp.float32
 ROW_BLOCKS = 2
+HOSTS = (0, 2, 4, 6, 8, 10, 12, 1)
 
 
 def host_tables(order):
@@ -114,22 +115,33 @@
 ):
     slots, n = measured_hbm.shape[0], measured_hbm.shape[1]
     wide = contrast_hbm.shape[3]
-    stride = n_beam // slots
     me = lax.axis_index("beam")
     lat = lax.axis_index("lat")
     before, after = lat - 1, lat + 1
     has_before, has_after = lat > 0, lat < n_lat - 1
 
     def hosts(i):
-        return lax.rem(i, stride) == 0
+        found = i == HOSTS[0]
+        for h in HOSTS[1:]:
+            found = found | (i == h)
+        return found
 
     def slot_of(i):
-        return i // stride
+        found = 0
+        for j, h in enumerate(HOSTS):
+            found = jnp.where(i == h, j, found)
+        return found
 
     def host(j):
-        return j * stride
-
-    lower = jnp.where(hosts(me), me, (me + stride - 1) // stride)
+        found = HOSTS[0]
+        for other, h in enumerate(HOSTS):
+            found = jnp.where(j == other, h, found)
+        return found
+
+    below = 0
+    for h in HOSTS:
+        below = below + jnp.where(h < me, 1, 0)
+    lower = jnp.where(hosts(me), me, below)
     works = hosts(me)
     slot = slot_of(me)
 
@@ -163,16 +175,17 @@
         ext[part, 0:n] = contrast[part, 0].astype(BF16)
     pl.semaphore_wait(barrier, lower + jnp.where(has_before & has_after, 2, 1))
 
+    low = n // 2
     rims = [
         pltpu.make_async_remote_copy(
-            src_ref=ext.at[part, 0:n],
-            dst_ref=ext.at[part, n : 2 * n],
-            send_sem=rim_send.at[part],
-            recv_sem=rim_recv.at[part],
+            src_ref=ext.at[:, h * low : (h + 1) * low],
+            dst_ref=ext.at[:, n + h * low : n + (h + 1) * low],
+            send_sem=rim_send.at[h],
+            recv_sem=rim_recv.at[h],
             device_id={"lat": before},
             device_id_type=MESH,
         )
-        for part in (0, 1)
+        for h in (0, 1)
     ]
 
     @pl.when(has_before)
@@ -194,7 +207,7 @@
     @pl.loop(0, slots)
     def _(j):
         x, y = ox_ref[j], oy_ref[j]
-        cut_rows[j] = picks((n, 2 * n), x, 1)
+        cut_rows[j] = picks((low, low + n), x, 1)
         cut_columns[j] = picks((wide, n), y, 0)
         put_columns[j] = picks((n, wide), y, 1)
         put_rows[j, 0] = picks((n, n), x, 0)
@@ -210,30 +223,49 @@
             device_id_type=MESH,
         )
 
+    def half_copy(j, h):
+        rows = slice(h * low, (h + 1) * low)
+        return pltpu.make_async_remote_copy(
+            src_ref=blocks.at[j, :, rows],
+            dst_ref=trans.at[me, :, rows],
+            send_sem=block_send.at[j],
+            recv_sem=block_recv.at[me],
+            device_id={"beam": host(j)},
+            device_id_type=MESH,
+        )
+
     group = 4
-    for part in (0, 1):
+    for h in (0, 1):
+        rows = slice(h * low, (h + 1) * low)
 
         @pl.when(has_after)
-        def _(part=part):
-            rims[part].wait_recv()
+        def _(h=h):
+            rims[h].wait_recv()
 
         @pl.when(jnp.logical_not(has_after))
-        def _(part=part):
-            ext[part, n : 2 * n] = jnp.zeros((n, wide), BF16)
+        def _(h=h):
+            ext[:, n + h * low : n + (h + 1) * low] = jnp.zeros((2, low, wide), BF16)
 
         @pl.loop(0, slots // group)
-        def _(g, part=part):
+        def _(g, h=h, rows=rows):
             members = [g * group + m for m in range(group)]
-            picked = [dot(cut_rows[j], ext[part]).astype(BF16) for j in members]
-            picked = [dot(p, cut_columns[j]).astype(BF16) for p, j in zip(picked, members)]
-            for p, j in zip(picked, members):
-                blocks[j, part] = p
-            if part == 1:
-                for j in members:
-
-                    @pl.when(host(j) < me)
-                    def _(j=j):
-                        block_copy(j).start()
+            lines = jnp.concatenate([cut_rows[j] for j in members], axis=0)
+            picked = [
+                dot(lines, ext[part, h * low : h * low + low + n]).astype(BF16) for part in (0, 1)
+            ]
+            for m, j in enumerate(members):
+                own = slice(m * low, (m + 1) * low)
+                both = jnp.concatenate([picked[0][own], picked[1][own]], axis=0)
+                both = dot(both, cut_columns[j]).astype(BF16)
+                blocks[j, 0, rows] = both[:low]
+                blocks[j, 1, rows] = both[low:]
+            for j in members:
+
+                @pl.when(host(j) < me)
+                def _(j=j):
+                    half_copy(j, h).start()
+
+                if h == 1:
 
                     @pl.when(host(j) == me)
                     def _(j=j):
@@ -420,7 +452,7 @@
             pltpu.VMEM(rights.shape, BF16),
             pltpu.VMEM(lefts.shape, BF16),
             pltpu.VMEM((2, 2 * n, wide), BF16),
-            pltpu.VMEM((slots, n, 2 * n), BF16),
+            pltpu.VMEM((slots, n // 2, n // 2 + n), BF16),
             pltpu.VMEM((slots, wide, n), BF16),
             pltpu.VMEM((slots, n, wide), BF16),
             pltpu.VMEM((slots, 2, n, n), BF16),

time: 66.6 us -> 66.3 us (level)
  the two profiles are of different devices: /device:TPU:10 before, /device:TPU:136 now
where the time goes in v4:
time: 66.3 us; the launch traced here: 66.1 us
  Pallas kernels  63.7 us (96%)
  other arithmetic  1.72 us (3%)
    pallas_call x1, Pallas kernels, on_device(): pl.pallas_call(functools.partial(kernel, n_beam=n_beam, n_lat=n_lat), out...  63.7 us
    add x1, other arithmetic, on_device(): return own + jnp.where(lax.axis_index('lat') > 0, rim.astype(F32), 0.0)  1.72 us

profile of v4, /device:TPU:136, one launch (start us, length us, event | category | flops | bytes accessed | tf_op | source)
XLA Modules:
  0.0 66.1 jit_solution(12866222366362146590)
XLA Ops:
  0.7 63.7 %shard_map.82 = (f32[2,1,128,256]{3,2,1,0:T(8,128)}, bf16[2,1,128,256]{3,2,1,0:T(8,128)(2,1)}) custom-call(s32[8]{0:T(128)} %ox_ref.1, s32[8]{0:T(128)} %oy_ref.1, s32[1]{0:T(128)S(6)} %copy.9.count_ref, f32[2,1,128,256]{3,2,1,0:T(8,128)} %contrast_hbm.1, f32[2,128,128]{2,1,0:T(8,128)} %probe_hbm.1, f32[8,128,128]{2,1,0:T(8,128)} %measured_hbm.1, ...), custom_call_target="tpu_custom_call" | custom-call | tf_op jit(solution)/shard_map/pallas_call | solution.py:441
  64.4 1.7 %select_add_fusion = f32[2,1,128,256]{3,2,1,0:T(8,128)} fusion(f32[2,1,128,256]{3,2,1,0:T(8,128)} %get-tuple-element.7, bf16[2,1,128,256]{3,2,1,0:T(8,128)(2,1)} %get-tuple-element.8, pred[]{:T(512)S(6)} %gt.3), kind=kLoop, calls=%fused_computation | loop fusion | flops 196608 | bytes 655361 | tf_op jit(solution)/shard_map/add | solution.py:484

commit v5 on v4

--- a/solution.py
+++ b/solution.py
@@ -188,16 +188,16 @@
         for h in (0, 1)
     ]
 
-    @pl.when(has_before)
-    def _():
-        for rim in rims:
-            rim.start()
-
     @pl.loop(0, me)
     def _(other):
         @pl.when(meets(me, other))
         def _():
             pl.semaphore_signal(here.at[me], inc=1, device_id={"beam": other}, device_id_type=MESH)
+
+    @pl.when(has_before)
+    def _():
+        for rim in rims:
+            rim.start()
 
     @pl.when(works)
     def _():

time: 66.3 us -> 66.3 us (level)
  no operation moved by 1% of the time
where the time goes in v5:
time: 66.3 us; the launch traced here: 66.1 us
  Pallas kernels  63.7 us (96%)
  other arithmetic  1.72 us (3%)
    pallas_call x1, Pallas kernels, on_device(): pl.pallas_call(functools.partial(kernel, n_beam=n_beam, n_lat=n_lat), out...  63.7 us
    add x1, other arithmetic, on_device(): return own + jnp.where(lax.axis_index('lat') > 0, rim.astype(F32), 0.0)  1.72 us

profile of v5, /device:TPU:136, one launch (start us, length us, event | category | flops | bytes accessed | tf_op | source)
XLA Modules:
  0.0 66.1 jit_solution(2945632652084776847)
XLA Ops:
  0.7 63.7 %shard_map.82 = (f32[2,1,128,256]{3,2,1,0:T(8,128)}, bf16[2,1,128,256]{3,2,1,0:T(8,128)(2,1)}) custom-call(s32[8]{0:T(128)} %ox_ref.1, s32[8]{0:T(128)} %oy_ref.1, s32[1]{0:T(128)S(6)} %copy.9.count_ref, f32[2,1,128,256]{3,2,1,0:T(8,128)} %contrast_hbm.1, f32[2,128,128]{2,1,0:T(8,128)} %probe_hbm.1, f32[8,128,128]{2,1,0:T(8,128)} %measured_hbm.1, ...), custom_call_target="tpu_custom_call" | custom-call | tf_op jit(solution)/shard_map/pallas_call | solution.py:441
  64.4 1.7 %select_add_fusion = f32[2,1,128,256]{3,2,1,0:T(8,128)} fusion(f32[2,1,128,256]{3,2,1,0:T(8,128)} %get-tuple-element.7, bf16[2,1,128,256]{3,2,1,0:T(8,128)(2,1)} %get-tuple-element.8, pred[]{:T(512)S(6)} %gt.3), kind=kLoop, calls=%fused_computation | loop fusion | flops 196608 | bytes 655361 | tf_op jit(solution)/shard_map/add | solution.py:484

commit v6 on v5

--- a/solution.py
+++ b/solution.py
@@ -234,7 +234,7 @@
             device_id_type=MESH,
         )
 
-    group = 4
+    group = 8
     for h in (0, 1):
         rows = slice(h * low, (h + 1) * low)
 

time: 66.3 us -> 66.5 us (level)
  no operation moved by 1% of the time
where the time goes in v6:
time: 66.5 us; the launch traced here: 66.3 us
  Pallas kernels  64 us (96%)
  other arithmetic  1.72 us (3%)
    pallas_call x1, Pallas kernels, on_device(): pl.pallas_call(functools.partial(kernel, n_beam=n_beam, n_lat=n_lat), out...  64 us
    add x1, other arithmetic, on_device(): return own + jnp.where(lax.axis_index('lat') > 0, rim.astype(F32), 0.0)  1.72 us

profile of v6, /device:TPU:136, one launch (start us, length us, event | category | flops | bytes accessed | tf_op | source)
XLA Modules:
  0.0 66.3 jit_solution(7315656228700148321)
XLA Ops:
  0.7 64.0 %shard_map.82 = (f32[2,1,128,256]{3,2,1,0:T(8,128)}, bf16[2,1,128,256]{3,2,1,0:T(8,128)(2,1)}) custom-call(s32[8]{0:T(128)} %ox_ref.1, s32[8]{0:T(128)} %oy_ref.1, s32[1]{0:T(128)S(6)} %copy.9.count_ref, f32[2,1,128,256]{3,2,1,0:T(8,128)} %contrast_hbm.1, f32[2,128,128]{2,1,0:T(8,128)} %probe_hbm.1, f32[8,128,128]{2,1,0:T(8,128)} %measured_hbm.1, ...), custom_call_target="tpu_custom_call" | custom-call | tf_op jit(solution)/shard_map/pallas_call | solution.py:441
  64.6 1.7 %select_add_fusion = f32[2,1,128,256]{3,2,1,0:T(8,128)} fusion(f32[2,1,128,256]{3,2,1,0:T(8,128)} %get-tuple-element.7, bf16[2,1,128,256]{3,2,1,0:T(8,128)(2,1)} %get-tuple-element.8, pred[]{:T(512)S(6)} %gt.3), kind=kLoop, calls=%fused_computation | loop fusion | flops 196608 | bytes 655361 | tf_op jit(solution)/shard_map/add | solution.py:484
